TPU v7x, 512 devices: a whole 4x8x8 slice. The times are simulated.
512 devices in a mesh: pipe: 8 (over z), expert: 32 (over y, x), dp: 2 (over core).
Axes of the slice: x: 4, y: 8, z: 8, core: 2. Of those that a mesh axis runs over, the one named last changes fastest.
Arguments:
- saved: bfloat16 [1, 8, 8192, 2560], P(None, 'pipe', ('expert', 'dp')), may hold values from -6 to 6
- cotangent: bfloat16 [8192, 2560], P(('expert', 'dp'), 'pipe'), may hold values from -1.1953125 to 1.1953125
- routes: int32 [1, 8, 8192, 1], P(None, 'pipe', ('expert', 'dp')), may hold values from 0 to 7; in each aligned block of 16 rows (0 to 15, 16 to 31, ..., all dimensions but the last counted through in order) at most 2 rows name the same one
- w_gate: bfloat16 [1, 8, 8192, 2560], P(None, 'pipe', 'expert', 'dp'), may hold values from -0.125 to 0.125
- w_up: bfloat16 [1, 8, 8192, 2560], P(None, 'pipe', 'expert', 'dp'), may hold values from -0.125 to 0.125
- w_down: bfloat16 [1, 8, 8192, 2560], P(None, 'pipe', 'expert', 'dp'), may hold values from -0.0625 to 0.0625
Outputs:
- grad_gate: bfloat16 [1, 8, 8192, 2560], P(None, 'pipe', 'expert', 'dp')
- grad_up: bfloat16 [1, 8, 8192, 2560], P(None, 'pipe', 'expert', 'dp')
Inputs may be any that keep to these rules, and one draw needn't show every extreme that they name: In each aligned block of 16 rows of routes (one micro-batch of one device, rows taken in order over all leading dimensions) no expert is named more than 2 times.
All inputs are finite; a program needn't handle non-finite values.
Results may differ from a plain program's by a relative error of at most 0.017.
Values may be sent and summed in bfloat16 or wider, within the bound.
No kernel may reach another device: no remote copies, remote signals or barrier semaphores. Data moves between devices by JAX's collectives and lax.ppermute only.
A program may use at most 64 MiB of HBM per device.

v0:
```python
import jax
import jax.numpy as jnp
from jax import lax
from jax.sharding import PartitionSpec as P

GROUP = 4
MICRO = 8
epsilon = 1e-06


def shifted(block, axis, distance):
    devices = range(lax.axis_size(axis))
    route = [(i - distance, i) for i in devices if i - distance in devices]
    return lax.ppermute(block, axis, route)


def slot_tables(route_ids, experts, capacity):
    onehot = (route_ids[..., None] == jnp.arange(experts, dtype=jnp.int32)).astype(jnp.int32)
    ranking = jnp.sum((jnp.cumsum(onehot, axis=2) - onehot) * onehot, axis=3)
    slot_ids = route_ids * capacity + ranking
    positions = jnp.arange(experts * capacity, dtype=jnp.int32)[:, None]
    placing = (slot_ids[..., None, :] == positions).astype(jnp.bfloat16)
    return (placing, slot_ids)


def shards(saved, cotangent, routes, w_gate, w_up, w_down):
    sections = lax.axis_size("pipe")
    width_all = lax.axis_size("expert")
    section_index = lax.axis_index("pipe")
    stretches = saved.shape[0]
    tok_dev = saved.shape[2]
    tok_mb = tok_dev // MICRO
    experts = width_all // GROUP
    capacity = max(2, tok_mb // experts)
    period = sections + MICRO - 1
    slot_count = width_all * capacity
    head_grad = lax.all_gather(cotangent, "pipe", axis=1, tiled=True)
    feature_count = head_grad.shape[1]
    slabs = (
        lax.all_gather(w_gate, "dp", axis=3, tiled=True),
        lax.all_gather(w_up, "dp", axis=3, tiled=True),
        lax.all_gather(w_down, "dp", axis=3, tiled=True),
    )
    gate_w = slabs[0][:, 0]
    up_w = slabs[1][:, 0]
    down_w = slabs[2][:, 0]
    hidden = gate_w.shape[1]
    inputs_f = saved[:, 0].astype(jnp.float32).reshape(stretches, MICRO, tok_mb, feature_count)
    norm_scale = lax.rsqrt(jnp.mean(inputs_f * inputs_f, axis=3, keepdims=True) + epsilon)
    unit_f = inputs_f * norm_scale
    unit_b = unit_f.astype(jnp.bfloat16)
    route_ids = routes[:, 0, :, 0].reshape(stretches, MICRO, tok_mb)
    placing, slot_ids = slot_tables(route_ids, experts, capacity)
    unit_slots = jnp.einsum("vmst,vmtd->vmsd", placing, unit_b, preferred_element_type=jnp.float32)
    unit_slots = unit_slots.astype(jnp.bfloat16).reshape(
        stretches, MICRO, experts, capacity, feature_count
    )
    unit_send = jnp.repeat(unit_slots, GROUP, axis=2)
    unit_recv = lax.all_to_all(unit_send, "expert", split_axis=2, concat_axis=2, tiled=True)
    unit_rows = unit_recv.reshape(stretches, MICRO, slot_count, feature_count)
    top_section = section_index == sections - 1

    def tick_step(tick_index, loop_state):
        carried, gate_store, up_store = loop_state
        stretch_index = 0
        micro_raw = tick_index - (sections - 1 - section_index)
        active = (micro_raw >= 0) & (micro_raw < MICRO)
        micro_index = jnp.clip(micro_raw, 0, MICRO - 1)
        seed_rows = lax.dynamic_slice_in_dim(head_grad, micro_index * tok_mb, tok_mb, 0)
        grad_in = jnp.where(top_section, seed_rows, carried)
        grad_in = jnp.where(active, grad_in, jnp.zeros_like(grad_in))
        place_now = placing[stretch_index, micro_index].reshape(experts, capacity, tok_mb)
        slot_grads = jnp.einsum(
            "ect,td->ecd", place_now, grad_in, preferred_element_type=jnp.float32
        )
        sending = jnp.repeat(slot_grads.astype(jnp.bfloat16), GROUP, axis=0)
        grad_rows = lax.all_to_all(
            sending, "expert", split_axis=0, concat_axis=0, tiled=True
        ).reshape(slot_count, feature_count)
        gate_slab = gate_w[stretch_index]
        up_slab = up_w[stretch_index]
        down_slab = down_w[stretch_index]
        unit_now = unit_rows[stretch_index, micro_index]
        gate = jnp.einsum("rd,hd->rh", unit_now, gate_slab, preferred_element_type=jnp.float32)
        up = jnp.einsum("rd,hd->rh", unit_now, up_slab, preferred_element_type=jnp.float32)
        hidden_grad = jnp.einsum(
            "rd,hd->rh", grad_rows, down_slab, preferred_element_type=jnp.float32
        )
        sigmoid_gate = jax.nn.sigmoid(gate)
        gate_grad = (hidden_grad * up * sigmoid_gate * (1.0 + gate * (1.0 - sigmoid_gate))).astype(
            jnp.bfloat16
        )
        up_grad = (hidden_grad * gate * sigmoid_gate).astype(jnp.bfloat16)
        partial_value = jnp.dot(gate_grad, gate_slab, preferred_element_type=jnp.float32)
        partial_value = (
            partial_value + jnp.dot(up_grad, up_slab, preferred_element_type=jnp.float32)
        ).astype(jnp.bfloat16)
        returned = lax.all_to_all(
            partial_value.reshape(width_all, capacity, feature_count),
            "expert",
            split_axis=0,
            concat_axis=0,
            tiled=True,
        )
        summed = (
            returned.reshape(experts, GROUP, capacity, feature_count)
            .astype(jnp.float32)
            .sum(axis=1)
        )
        unit_grad = jnp.take(
            summed.reshape(experts * capacity, feature_count),
            slot_ids[stretch_index, micro_index],
            axis=0,
        )
        unit_here = unit_f[stretch_index, micro_index]
        scale_rows = norm_scale[stretch_index, micro_index]
        norm_grad = scale_rows * (
            unit_grad - unit_here * jnp.mean(unit_grad * unit_here, axis=1, keepdims=True)
        )
        grad_out = (grad_in.astype(jnp.float32) + norm_grad).astype(jnp.bfloat16)
        carried = shifted(grad_out, "pipe", -1)
        gate_store = jnp.where(
            active, gate_store.at[stretch_index, micro_index].set(gate_grad), gate_store
        )
        up_store = jnp.where(active, up_store.at[stretch_index, micro_index].set(up_grad), up_store)
        return (carried, gate_store, up_store)

    start_state = (
        jnp.zeros((tok_mb, feature_count), jnp.bfloat16),
        jnp.zeros((stretches, MICRO, slot_count, hidden), jnp.bfloat16),
        jnp.zeros((stretches, MICRO, slot_count, hidden), jnp.bfloat16),
    )
    final_state = lax.fori_loop(0, period, tick_step, start_state)
    flat_units = unit_rows.reshape(stretches, MICRO * slot_count, feature_count)
    part_gate = jnp.einsum(
        "vrh,vrd->vhd",
        final_state[1].reshape(stretches, MICRO * slot_count, hidden),
        flat_units,
        preferred_element_type=jnp.float32,
    )
    part_up = jnp.einsum(
        "vrh,vrd->vhd",
        final_state[2].reshape(stretches, MICRO * slot_count, hidden),
        flat_units,
        preferred_element_type=jnp.float32,
    )
    totals = (
        lax.psum_scatter(
            part_gate.astype(jnp.bfloat16), "dp", scatter_dimension=2, tiled=True
        ).astype(jnp.float32),
        lax.psum_scatter(
            part_up.astype(jnp.bfloat16), "dp", scatter_dimension=2, tiled=True
        ).astype(jnp.float32),
    )
    grad_gate = totals[0].astype(jnp.bfloat16)[:, None]
    grad_up = totals[1].astype(jnp.bfloat16)[:, None]
    return (grad_gate, grad_up)


def solution(mesh):
    in_specs = (
        P(None, "pipe", ("expert", "dp"), None),
        P(("expert", "dp"), "pipe"),
        P(None, "pipe", ("expert", "dp"), None),
        P(None, "pipe", "expert", "dp"),
        P(None, "pipe", "expert", "dp"),
        P(None, "pipe", "expert", "dp"),
    )
    out_specs = (P(None, "pipe", "expert", "dp"), P(None, "pipe", "expert", "dp"))
    return jax.shard_map(shards, mesh=mesh, in_specs=in_specs, out_specs=out_specs, check_vma=False)
```

profile of v0, /device:TPU:1, one launch (start us, length us, event | category | flops | bytes accessed | tf_op | source)
XLA Modules:
  0.0 954.3 jit_solution(4917801500919075737)
XLA Ops:
  12.8 4.0 broadcast_in_dim.60
  16.8 10.5 %all-to-all-start.2 = ((bf16[1,8,32,2,2560]{4,3,1,0,2:T(2,128)(2,1)}), bf16[1,8,32,2,2560]{4,3,1,0,2:T(2,128)(2,1)S(1)}, u32[]{:S(2)}, u32[]{:S(2)}) async-start(bf16[1,8,32,2,2560]{4,3,1,0,2:T(2,128)(2,1)} %bitcast.139), calls=%async_computation.2 | async-start | bytes 5242880 | tf_op jit(solution)/shard_map/all_to_all | solution.py:59
  29.6 28.2 %all_gather.12 = bf16[128,2560]{0,1:T(8,128)(2,1)S(1)} all-gather(bf16[128,320]{0,1:T(8,128)(2,1)S(1)} %copy-done.6), channel_id=1, replica_groups=mesh['pipe'=8,'expert'=32,'dp'=2] {'pipe'}, dimensions={1}, use_global_device_ids=true | all-gather | bytes 737280 | tf_op jit(solution)/shard_map/all_gather | solution.py:37
  61.6 25.4 %all-to-all-done.2 = bf16[1,8,32,2,2560]{4,3,1,0,2:T(2,128)(2,1)S(1)} async-done(((bf16[1,8,32,2,2560]{4,3,1,0,2:T(2,128)(2,1)}), bf16[1,8,32,2,2560]{4,3,1,0,2:T(2,128)(2,1)S(1)}, u32[]{:S(2)}, u32[]{:S(2)}) %all-to-all-start.2) | async-done | bytes 2621472 | tf_op jit(solution)/shard_map/all_to_all | solution.py:59
  93.1 6.7 reshape.422
  101.3 753.9 %while.21 = (s32[]{:T(128)}, bf16[16,2560]{1,0:T(8,128)(2,1)S(1)}, bf16[1,8,64,256]{3,2,1,0:T(8,128)(2,1)}, bf16[1,8,64,256]{3,2,1,0:T(8,128)(2,1)}, s32[]{:T(12...) while((s32[]{:T(128)}, bf16[16,2560]{1,0:T(8,128)(2,1)S(1)}, ...), condition=%wide.region_7.8_spmd, body=%wide.region_3.7_spmd.sunk | while | flops 422298752 | bytes 31975776 | solution.py:133
  103.4 6.9 all-to-all-start
  111.0 10.5 %all-to-all-done = bf16[32,2,2560]{2,1,0:T(2,128)(2,1)S(1)} async-done(((bf16[32,2,2560]{2,1,0:T(2,128)(2,1)}), bf16[32,2,2560]{2,1,0:T(2,128)(2,1)S(1)}, u32[]{:S(2)}, u32[]{:S(2)}) %all-to-all-start) | async-done | bytes 327712 | tf_op jit(solution)/shard_map/while/body/eval_jaxpr/all_to_all | solution.py:77
  129.3 5.9 all-to-all-start.1
  135.3 10.7 %all-to-all-done.1 = bf16[32,2,2560]{2,1,0:T(2,128)(2,1)S(1)} async-done(((bf16[32,2,2560]{2,1,0:T(2,128)(2,1)}), bf16[32,2,2560]{2,1,0:T(2,128)(2,1)S(1)}, u32[]{:S(2)}, u32[]{:S(2)}) %all-to-all-start.1) | async-done | bytes 327712 | tf_op jit(solution)/shard_map/while/body/eval_jaxpr/all_to_all | solution.py:98
  150.6 4.4 collective-permute-done
  157.1 6.2 all-to-all-start
  164.0 10.1 %all-to-all-done = bf16[32,2,2560]{2,1,0:T(2,128)(2,1)S(1)} async-done(((bf16[32,2,2560]{2,1,0:T(2,128)(2,1)}), bf16[32,2,2560]{2,1,0:T(2,128)(2,1)S(1)}, u32[]{:S(2)}, u32[]{:S(2)}) %all-to-all-start) | async-done | bytes 327712 | tf_op jit(solution)/shard_map/while/body/eval_jaxpr/all_to_all | solution.py:77
  181.9 4.3 all-to-all-start.1
  186.3 10.7 %all-to-all-done.1 = bf16[32,2,2560]{2,1,0:T(2,128)(2,1)S(1)} async-done(((bf16[32,2,2560]{2,1,0:T(2,128)(2,1)}), bf16[32,2,2560]{2,1,0:T(2,128)(2,1)S(1)}, u32[]{:S(2)}, u32[]{:S(2)}) %all-to-all-start.1) | async-done | bytes 327712 | tf_op jit(solution)/shard_map/while/body/eval_jaxpr/all_to_all | solution.py:98
  201.5 4.6 collective-permute-done
  208.2 4.2 all-to-all-start
  213.1 10.0 %all-to-all-done = bf16[32,2,2560]{2,1,0:T(2,128)(2,1)S(1)} async-done(((bf16[32,2,2560]{2,1,0:T(2,128)(2,1)}), bf16[32,2,2560]{2,1,0:T(2,128)(2,1)S(1)}, u32[]{:S(2)}, u32[]{:S(2)}) %all-to-all-start) | async-done | bytes 327712 | tf_op jit(solution)/shard_map/while/body/eval_jaxpr/all_to_all | solution.py:77
  230.8 4.0 all-to-all-start.1
  234.9 10.6 %all-to-all-done.1 = bf16[32,2,2560]{2,1,0:T(2,128)(2,1)S(1)} async-done(((bf16[32,2,2560]{2,1,0:T(2,128)(2,1)}), bf16[32,2,2560]{2,1,0:T(2,128)(2,1)S(1)}, u32[]{:S(2)}, u32[]{:S(2)}) %all-to-all-start.1) | async-done | bytes 327712 | tf_op jit(solution)/shard_map/while/body/eval_jaxpr/all_to_all | solution.py:98
  250.1 4.5 collective-permute-done
  261.4 10.0 %all-to-all-done = bf16[32,2,2560]{2,1,0:T(2,128)(2,1)S(1)} async-done(((bf16[32,2,2560]{2,1,0:T(2,128)(2,1)}), bf16[32,2,2560]{2,1,0:T(2,128)(2,1)S(1)}, u32[]{:S(2)}, u32[]{:S(2)}) %all-to-all-start) | async-done | bytes 327712 | tf_op jit(solution)/shard_map/while/body/eval_jaxpr/all_to_all | solution.py:77
  283.1 10.6 %all-to-all-done.1 = bf16[32,2,2560]{2,1,0:T(2,128)(2,1)S(1)} async-done(((bf16[32,2,2560]{2,1,0:T(2,128)(2,1)}), bf16[32,2,2560]{2,1,0:T(2,128)(2,1)S(1)}, u32[]{:S(2)}, u32[]{:S(2)}) %all-to-all-start.1) | async-done | bytes 327712 | tf_op jit(solution)/shard_map/while/body/eval_jaxpr/all_to_all | solution.py:98
  298.3 6.0 collective-permute-done
  306.5 3.9 all-to-all-start
  311.2 10.0 %all-to-all-done = bf16[32,2,2560]{2,1,0:T(2,128)(2,1)S(1)} async-done(((bf16[32,2,2560]{2,1,0:T(2,128)(2,1)}), bf16[32,2,2560]{2,1,0:T(2,128)(2,1)S(1)}, u32[]{:S(2)}, u32[]{:S(2)}) %all-to-all-start) | async-done | bytes 327712 | tf_op jit(solution)/shard_map/while/body/eval_jaxpr/all_to_all | solution.py:77
  332.9 10.6 %all-to-all-done.1 = bf16[32,2,2560]{2,1,0:T(2,128)(2,1)S(1)} async-done(((bf16[32,2,2560]{2,1,0:T(2,128)(2,1)}), bf16[32,2,2560]{2,1,0:T(2,128)(2,1)S(1)}, u32[]{:S(2)}, u32[]{:S(2)}) %all-to-all-start.1) | async-done | bytes 327712 | tf_op jit(solution)/shard_map/while/body/eval_jaxpr/all_to_all | solution.py:98
  348.1 5.4 collective-permute-done
  355.6 3.9 all-to-all-start
  360.3 10.0 %all-to-all-done = bf16[32,2,2560]{2,1,0:T(2,128)(2,1)S(1)} async-done(((bf16[32,2,2560]{2,1,0:T(2,128)(2,1)}), bf16[32,2,2560]{2,1,0:T(2,128)(2,1)S(1)}, u32[]{:S(2)}, u32[]{:S(2)}) %all-to-all-start) | async-done | bytes 327712 | tf_op jit(solution)/shard_map/while/body/eval_jaxpr/all_to_all | solution.py:77
  382.0 11.0 %all-to-all-done.1 = bf16[32,2,2560]{2,1,0:T(2,128)(2,1)S(1)} async-done(((bf16[32,2,2560]{2,1,0:T(2,128)(2,1)}), bf16[32,2,2560]{2,1,0:T(2,128)(2,1)S(1)}, u32[]{:S(2)}, u32[]{:S(2)}) %all-to-all-start.1) | async-done | bytes 327712 | tf_op jit(solution)/shard_map/while/body/eval_jaxpr/all_to_all | solution.py:98
  397.5 5.0 collective-permute-done
  409.2 10.5 %all-to-all-done = bf16[32,2,2560]{2,1,0:T(2,128)(2,1)S(1)} async-done(((bf16[32,2,2560]{2,1,0:T(2,128)(2,1)}), bf16[32,2,2560]{2,1,0:T(2,128)(2,1)S(1)}, u32[]{:S(2)}, u32[]{:S(2)}) %all-to-all-start) | async-done | bytes 327712 | tf_op jit(solution)/shard_map/while/body/eval_jaxpr/all_to_all | solution.py:77
  431.3 12.4 %all-to-all-done.1 = bf16[32,2,2560]{2,1,0:T(2,128)(2,1)S(1)} async-done(((bf16[32,2,2560]{2,1,0:T(2,128)(2,1)}), bf16[32,2,2560]{2,1,0:T(2,128)(2,1)S(1)}, u32[]{:S(2)}, u32[]{:S(2)}) %all-to-all-start.1) | async-done | bytes 327712 | tf_op jit(solution)/shard_map/while/body/eval_jaxpr/all_to_all | solution.py:98
  448.3 5.6 collective-permute-done
  460.5 10.3 %all-to-all-done = bf16[32,2,2560]{2,1,0:T(2,128)(2,1)S(1)} async-done(((bf16[32,2,2560]{2,1,0:T(2,128)(2,1)}), bf16[32,2,2560]{2,1,0:T(2,128)(2,1)S(1)}, u32[]{:S(2)}, u32[]{:S(2)}) %all-to-all-start) | async-done | bytes 327712 | tf_op jit(solution)/shard_map/while/body/eval_jaxpr/all_to_all | solution.py:77
  482.5 11.1 %all-to-all-done.1 = bf16[32,2,2560]{2,1,0:T(2,128)(2,1)S(1)} async-done(((bf16[32,2,2560]{2,1,0:T(2,128)(2,1)}), bf16[32,2,2560]{2,1,0:T(2,128)(2,1)S(1)}, u32[]{:S(2)}, u32[]{:S(2)}) %all-to-all-start.1) | async-done | bytes 327712 | tf_op jit(solution)/shard_map/while/body/eval_jaxpr/all_to_all | solution.py:98
  498.1 5.3 collective-permute-done
  505.6 5.8 all-to-all-start
  512.0 12.4 %all-to-all-done = bf16[32,2,2560]{2,1,0:T(2,128)(2,1)S(1)} async-done(((bf16[32,2,2560]{2,1,0:T(2,128)(2,1)}), bf16[32,2,2560]{2,1,0:T(2,128)(2,1)S(1)}, u32[]{:S(2)}, u32[]{:S(2)}) %all-to-all-start) | async-done | bytes 327712 | tf_op jit(solution)/shard_map/while/body/eval_jaxpr/all_to_all | solution.py:77
  536.1 11.1 %all-to-all-done.1 = bf16[32,2,2560]{2,1,0:T(2,128)(2,1)S(1)} async-done(((bf16[32,2,2560]{2,1,0:T(2,128)(2,1)}), bf16[32,2,2560]{2,1,0:T(2,128)(2,1)S(1)}, u32[]{:S(2)}, u32[]{:S(2)}) %all-to-all-start.1) | async-done | bytes 327712 | tf_op jit(solution)/shard_map/while/body/eval_jaxpr/all_to_all | solution.py:98
  551.8 5.4 collective-permute-done
  563.9 11.3 %all-to-all-done = bf16[32,2,2560]{2,1,0:T(2,128)(2,1)S(1)} async-done(((bf16[32,2,2560]{2,1,0:T(2,128)(2,1)}), bf16[32,2,2560]{2,1,0:T(2,128)(2,1)S(1)}, u32[]{:S(2)}, u32[]{:S(2)}) %all-to-all-start) | async-done | bytes 327712 | tf_op jit(solution)/shard_map/while/body/eval_jaxpr/all_to_all | solution.py:77
  582.9 5.1 all-to-all-start.1
  588.1 10.6 %all-to-all-done.1 = bf16[32,2,2560]{2,1,0:T(2,128)(2,1)S(1)} async-done(((bf16[32,2,2560]{2,1,0:T(2,128)(2,1)}), bf16[32,2,2560]{2,1,0:T(2,128)(2,1)S(1)}, u32[]{:S(2)}, u32[]{:S(2)}) %all-to-all-start.1) | async-done | bytes 327712 | tf_op jit(solution)/shard_map/while/body/eval_jaxpr/all_to_all | solution.py:98
  603.4 5.1 collective-permute-done
  615.2 10.0 %all-to-all-done = bf16[32,2,2560]{2,1,0:T(2,128)(2,1)S(1)} async-done(((bf16[32,2,2560]{2,1,0:T(2,128)(2,1)}), bf16[32,2,2560]{2,1,0:T(2,128)(2,1)S(1)}, u32[]{:S(2)}, u32[]{:S(2)}) %all-to-all-start) | async-done | bytes 327712 | tf_op jit(solution)/shard_map/while/body/eval_jaxpr/all_to_all | solution.py:77
  632.9 4.0 all-to-all-start.1
  637.0 10.6 %all-to-all-done.1 = bf16[32,2,2560]{2,1,0:T(2,128)(2,1)S(1)} async-done(((bf16[32,2,2560]{2,1,0:T(2,128)(2,1)}), bf16[32,2,2560]{2,1,0:T(2,128)(2,1)S(1)}, u32[]{:S(2)}, u32[]{:S(2)}) %all-to-all-start.1) | async-done | bytes 327712 | tf_op jit(solution)/shard_map/while/body/eval_jaxpr/all_to_all | solution.py:98
  652.2 5.5 collective-permute-done
  664.5 10.0 %all-to-all-done = bf16[32,2,2560]{2,1,0:T(2,128)(2,1)S(1)} async-done(((bf16[32,2,2560]{2,1,0:T(2,128)(2,1)}), bf16[32,2,2560]{2,1,0:T(2,128)(2,1)S(1)}, u32[]{:S(2)}, u32[]{:S(2)}) %all-to-all-start) | async-done | bytes 327712 | tf_op jit(solution)/shard_map/while/body/eval_jaxpr/all_to_all | solution.py:77
  686.3 10.6 %all-to-all-done.1 = bf16[32,2,2560]{2,1,0:T(2,128)(2,1)S(1)} async-done(((bf16[32,2,2560]{2,1,0:T(2,128)(2,1)}), bf16[32,2,2560]{2,1,0:T(2,128)(2,1)S(1)}, u32[]{:S(2)}, u32[]{:S(2)}) %all-to-all-start.1) | async-done | bytes 327712 | tf_op jit(solution)/shard_map/while/body/eval_jaxpr/all_to_all | solution.py:98
  701.5 5.2 collective-permute-done
  713.4 10.0 %all-to-all-done = bf16[32,2,2560]{2,1,0:T(2,128)(2,1)S(1)} async-done(((bf16[32,2,2560]{2,1,0:T(2,128)(2,1)}), bf16[32,2,2560]{2,1,0:T(2,128)(2,1)S(1)}, u32[]{:S(2)}, u32[]{:S(2)}) %all-to-all-start) | async-done | bytes 327712 | tf_op jit(solution)/shard_map/while/body/eval_jaxpr/all_to_all | solution.py:77
  735.1 10.6 %all-to-all-done.1 = bf16[32,2,2560]{2,1,0:T(2,128)(2,1)S(1)} async-done(((bf16[32,2,2560]{2,1,0:T(2,128)(2,1)}), bf16[32,2,2560]{2,1,0:T(2,128)(2,1)S(1)}, u32[]{:S(2)}, u32[]{:S(2)}) %all-to-all-start.1) | async-done | bytes 327712 | tf_op jit(solution)/shard_map/while/body/eval_jaxpr/all_to_all | solution.py:98
  750.3 5.2 collective-permute-done
  762.3 10.0 %all-to-all-done = bf16[32,2,2560]{2,1,0:T(2,128)(2,1)S(1)} async-done(((bf16[32,2,2560]{2,1,0:T(2,128)(2,1)}), bf16[32,2,2560]{2,1,0:T(2,128)(2,1)S(1)}, u32[]{:S(2)}, u32[]{:S(2)}) %all-to-all-start) | async-done | bytes 327712 | tf_op jit(solution)/shard_map/while/body/eval_jaxpr/all_to_all | solution.py:77
  784.1 10.6 %all-to-all-done.1 = bf16[32,2,2560]{2,1,0:T(2,128)(2,1)S(1)} async-done(((bf16[32,2,2560]{2,1,0:T(2,128)(2,1)}), bf16[32,2,2560]{2,1,0:T(2,128)(2,1)S(1)}, u32[]{:S(2)}, u32[]{:S(2)}) %all-to-all-start.1) | async-done | bytes 327712 | tf_op jit(solution)/shard_map/while/body/eval_jaxpr/all_to_all | solution.py:98
  799.3 5.0 collective-permute-done
  811.0 10.3 %all-to-all-done = bf16[32,2,2560]{2,1,0:T(2,128)(2,1)S(1)} async-done(((bf16[32,2,2560]{2,1,0:T(2,128)(2,1)}), bf16[32,2,2560]{2,1,0:T(2,128)(2,1)S(1)}, u32[]{:S(2)}, u32[]{:S(2)}) %all-to-all-start) | async-done | bytes 327712 | tf_op jit(solution)/shard_map/while/body/eval_jaxpr/all_to_all | solution.py:77
  833.0 11.8 %all-to-all-done.1 = bf16[32,2,2560]{2,1,0:T(2,128)(2,1)S(1)} async-done(((bf16[32,2,2560]{2,1,0:T(2,128)(2,1)}), bf16[32,2,2560]{2,1,0:T(2,128)(2,1)S(1)}, u32[]{:S(2)}, u32[]{:S(2)}) %all-to-all-start.1) | async-done | bytes 327712 | tf_op jit(solution)/shard_map/while/body/eval_jaxpr/all_to_all | solution.py:98
  849.4 5.8 collective-permute-done
  862.0 64.3 %reduce-scatter.5.cloned.1.call-done = bf16[1,256,1280]{2,1,0:T(8,128)(2,1)} async-done(((bf16[1,256,2560]{2,1,0:T(8,128)(2,1)}), bf16[1,256,1280]{2,1,0:T(8,128)(2,1)}) %reduce-scatter.5.cloned.1.call-update) | async-done | bytes 655376 | tf_op jit(solution)/shard_map/reduce_scatter | solution.py:151
  926.3 21.4 %reduce-scatter.3.cloned.1.call-done = bf16[1,256,1280]{2,1,0:T(8,128)(2,1)} async-done(((bf16[1,256,2560]{2,1,0:T(8,128)(2,1)}), bf16[1,256,1280]{2,1,0:T(8,128)(2,1)}) %reduce-scatter.3.cloned.1.call-update) | async-done | bytes 655376 | tf_op jit(solution)/shard_map/reduce_scatter | solution.py:148
  (507 shorter events, 326.2 us)
Async XLA Ops:
  16.8 70.2 %all-to-all-start.2 = ((bf16[1,8,32,2,2560]{4,3,1,0,2:T(2,128)(2,1)}), bf16[1,8,32,2,2560]{4,3,1,0,2:T(2,128)(2,1)S(1)}, u32[]{:S(2)}, u32[]{:S(2)}) async-start(bf16[1,8,32,2,2560]{4,3,1,0,2:T(2,128)(2,1)} %bitcast.139), calls=%async_computation.2 | async-start | bytes 5242880 | tf_op jit(solution)/shard_map/all_to_all | solution.py:59
  27.3 72.5 %all-gather.4.cloned.1.call-start = ((), (), s32[]{:S(2)}) async-start(), calls=%async_computation.5 | async-start | bytes 1966080 | tf_op jit(solution)/shard_map/all_gather | solution.py:42
  28.0 71.8 %all-gather.6.cloned.1.call-start = ((), (), s32[]{:S(2)}) async-start(), calls=%async_computation.6 | async-start | bytes 1966080 | tf_op jit(solution)/shard_map/all_gather | solution.py:41
  28.8 71.1 %all-gather.8.cloned.1.call-start = ((), (), s32[]{:S(2)}) async-start(), calls=%async_computation.7 | async-start | bytes 1966080 | tf_op jit(solution)/shard_map/all_gather | solution.py:40
  29.5 896.8 %reduce-scatter.5.cloned.1.call-start = ((), (), s32[]{:S(2)}) async-start(), calls=%async_computation.9 | async-start | bytes 1966080 | tf_op jit(solution)/shard_map/reduce_scatter | solution.py:151
  101.3 20.4 %copy-start.2 = (bf16[1,1,256,2560]{3,2,1,0:T(8,128)(2,1)S(1)}, bf16[1,1,256,2560]{3,2,1,0:T(8,128)(2,1)}, u32[]{:S(2)}) copy-start(bf16[1,1,256,2560]{3,2,1,0:T(8,128)(2,1)} %get-tuple-element.656) | copy-start | bytes 3932164 | tf_op jit(solution)/shard_map/while
  103.4 18.2 %all-to-all-start = ((bf16[32,2,2560]{2,1,0:T(2,128)(2,1)}), bf16[32,2,2560]{2,1,0:T(2,128)(2,1)S(1)}, u32[]{:S(2)}, u32[]{:S(2)}) async-start(bf16[32,2,2560]{2,1,0:T(2,128)(2,1)} %bitcast.136), calls=%async_computation | async-start | bytes 655360 | tf_op jit(solution)/shard_map/while/body/eval_jaxpr/all_to_all | solution.py:77
  129.3 16.7 %all-to-all-start.1 = ((bf16[32,2,2560]{2,1,0:T(2,128)(2,1)}), bf16[32,2,2560]{2,1,0:T(2,128)(2,1)S(1)}, u32[]{:S(2)}, u32[]{:S(2)}) async-start(bf16[32,2,2560]{2,1,0:T(2,128)(2,1)} %reshape.458), calls=%async_computation.1 | async-start | bytes 655360 | tf_op jit(solution)/shard_map/while/body/eval_jaxpr/all_to_all | solution.py:98
  149.2 5.7 collective-permute-start
  155.0 19.3 %copy-start.2 = (bf16[1,1,256,2560]{3,2,1,0:T(8,128)(2,1)S(1)}, bf16[1,1,256,2560]{3,2,1,0:T(8,128)(2,1)}, u32[]{:S(2)}) copy-start(bf16[1,1,256,2560]{3,2,1,0:T(8,128)(2,1)} %get-tuple-element.656) | copy-start | bytes 3932164 | tf_op jit(solution)/shard_map/while
  157.1 17.1 %all-to-all-start = ((bf16[32,2,2560]{2,1,0:T(2,128)(2,1)}), bf16[32,2,2560]{2,1,0:T(2,128)(2,1)S(1)}, u32[]{:S(2)}, u32[]{:S(2)}) async-start(bf16[32,2,2560]{2,1,0:T(2,128)(2,1)} %bitcast.136), calls=%async_computation | async-start | bytes 655360 | tf_op jit(solution)/shard_map/while/body/eval_jaxpr/all_to_all | solution.py:77
  181.9 15.0 %all-to-all-start.1 = ((bf16[32,2,2560]{2,1,0:T(2,128)(2,1)}), bf16[32,2,2560]{2,1,0:T(2,128)(2,1)S(1)}, u32[]{:S(2)}, u32[]{:S(2)}) async-start(bf16[32,2,2560]{2,1,0:T(2,128)(2,1)} %reshape.458), calls=%async_computation.1 | async-start | bytes 655360 | tf_op jit(solution)/shard_map/while/body/eval_jaxpr/all_to_all | solution.py:98
  200.2 5.9 collective-permute-start
  206.1 17.2 %copy-start.2 = (bf16[1,1,256,2560]{3,2,1,0:T(8,128)(2,1)S(1)}, bf16[1,1,256,2560]{3,2,1,0:T(8,128)(2,1)}, u32[]{:S(2)}) copy-start(bf16[1,1,256,2560]{3,2,1,0:T(8,128)(2,1)} %get-tuple-element.656) | copy-start | bytes 3932164 | tf_op jit(solution)/shard_map/while
  208.2 14.9 %all-to-all-start = ((bf16[32,2,2560]{2,1,0:T(2,128)(2,1)}), bf16[32,2,2560]{2,1,0:T(2,128)(2,1)S(1)}, u32[]{:S(2)}, u32[]{:S(2)}) async-start(bf16[32,2,2560]{2,1,0:T(2,128)(2,1)} %bitcast.136), calls=%async_computation | async-start | bytes 655360 | tf_op jit(solution)/shard_map/while/body/eval_jaxpr/all_to_all | solution.py:77
  230.8 14.7 %all-to-all-start.1 = ((bf16[32,2,2560]{2,1,0:T(2,128)(2,1)}), bf16[32,2,2560]{2,1,0:T(2,128)(2,1)S(1)}, u32[]{:S(2)}, u32[]{:S(2)}) async-start(bf16[32,2,2560]{2,1,0:T(2,128)(2,1)} %reshape.458), calls=%async_computation.1 | async-start | bytes 655360 | tf_op jit(solution)/shard_map/while/body/eval_jaxpr/all_to_all | solution.py:98
  248.8 5.8 collective-permute-start
  254.6 16.9 %copy-start.2 = (bf16[1,1,256,2560]{3,2,1,0:T(8,128)(2,1)S(1)}, bf16[1,1,256,2560]{3,2,1,0:T(8,128)(2,1)}, u32[]{:S(2)}) copy-start(bf16[1,1,256,2560]{3,2,1,0:T(8,128)(2,1)} %get-tuple-element.656) | copy-start | bytes 3932164 | tf_op jit(solution)/shard_map/while
  256.7 14.7 %all-to-all-start = ((bf16[32,2,2560]{2,1,0:T(2,128)(2,1)}), bf16[32,2,2560]{2,1,0:T(2,128)(2,1)S(1)}, u32[]{:S(2)}, u32[]{:S(2)}) async-start(bf16[32,2,2560]{2,1,0:T(2,128)(2,1)} %bitcast.136), calls=%async_computation | async-start | bytes 655360 | tf_op jit(solution)/shard_map/while/body/eval_jaxpr/all_to_all | solution.py:77
  279.1 14.7 %all-to-all-start.1 = ((bf16[32,2,2560]{2,1,0:T(2,128)(2,1)}), bf16[32,2,2560]{2,1,0:T(2,128)(2,1)S(1)}, u32[]{:S(2)}, u32[]{:S(2)}) async-start(bf16[32,2,2560]{2,1,0:T(2,128)(2,1)} %reshape.458), calls=%async_computation.1 | async-start | bytes 655360 | tf_op jit(solution)/shard_map/while/body/eval_jaxpr/all_to_all | solution.py:98
  297.0 7.3 collective-permute-start
  304.4 16.9 %copy-start.2 = (bf16[1,1,256,2560]{3,2,1,0:T(8,128)(2,1)S(1)}, bf16[1,1,256,2560]{3,2,1,0:T(8,128)(2,1)}, u32[]{:S(2)}) copy-start(bf16[1,1,256,2560]{3,2,1,0:T(8,128)(2,1)} %get-tuple-element.656) | copy-start | bytes 3932164 | tf_op jit(solution)/shard_map/while
  306.5 14.7 %all-to-all-start = ((bf16[32,2,2560]{2,1,0:T(2,128)(2,1)}), bf16[32,2,2560]{2,1,0:T(2,128)(2,1)S(1)}, u32[]{:S(2)}, u32[]{:S(2)}) async-start(bf16[32,2,2560]{2,1,0:T(2,128)(2,1)} %bitcast.136), calls=%async_computation | async-start | bytes 655360 | tf_op jit(solution)/shard_map/while/body/eval_jaxpr/all_to_all | solution.py:77
  328.9 14.7 %all-to-all-start.1 = ((bf16[32,2,2560]{2,1,0:T(2,128)(2,1)}), bf16[32,2,2560]{2,1,0:T(2,128)(2,1)S(1)}, u32[]{:S(2)}, u32[]{:S(2)}) async-start(bf16[32,2,2560]{2,1,0:T(2,128)(2,1)} %reshape.458), calls=%async_computation.1 | async-start | bytes 655360 | tf_op jit(solution)/shard_map/while/body/eval_jaxpr/all_to_all | solution.py:98
  346.8 6.7 collective-permute-start
  353.5 16.9 %copy-start.2 = (bf16[1,1,256,2560]{3,2,1,0:T(8,128)(2,1)S(1)}, bf16[1,1,256,2560]{3,2,1,0:T(8,128)(2,1)}, u32[]{:S(2)}) copy-start(bf16[1,1,256,2560]{3,2,1,0:T(8,128)(2,1)} %get-tuple-element.656) | copy-start | bytes 3932164 | tf_op jit(solution)/shard_map/while
  355.6 14.7 %all-to-all-start = ((bf16[32,2,2560]{2,1,0:T(2,128)(2,1)}), bf16[32,2,2560]{2,1,0:T(2,128)(2,1)S(1)}, u32[]{:S(2)}, u32[]{:S(2)}) async-start(bf16[32,2,2560]{2,1,0:T(2,128)(2,1)} %bitcast.136), calls=%async_computation | async-start | bytes 655360 | tf_op jit(solution)/shard_map/while/body/eval_jaxpr/all_to_all | solution.py:77
  378.0 15.0 %all-to-all-start.1 = ((bf16[32,2,2560]{2,1,0:T(2,128)(2,1)}), bf16[32,2,2560]{2,1,0:T(2,128)(2,1)S(1)}, u32[]{:S(2)}, u32[]{:S(2)}) async-start(bf16[32,2,2560]{2,1,0:T(2,128)(2,1)} %reshape.458), calls=%async_computation.1 | async-start | bytes 655360 | tf_op jit(solution)/shard_map/while/body/eval_jaxpr/all_to_all | solution.py:98
  396.2 6.3 collective-permute-start
  402.5 17.3 %copy-start.2 = (bf16[1,1,256,2560]{3,2,1,0:T(8,128)(2,1)S(1)}, bf16[1,1,256,2560]{3,2,1,0:T(8,128)(2,1)}, u32[]{:S(2)}) copy-start(bf16[1,1,256,2560]{3,2,1,0:T(8,128)(2,1)} %get-tuple-element.656) | copy-start | bytes 3932164 | tf_op jit(solution)/shard_map/while
  404.6 15.1 %all-to-all-start = ((bf16[32,2,2560]{2,1,0:T(2,128)(2,1)}), bf16[32,2,2560]{2,1,0:T(2,128)(2,1)S(1)}, u32[]{:S(2)}, u32[]{:S(2)}) async-start(bf16[32,2,2560]{2,1,0:T(2,128)(2,1)} %bitcast.136), calls=%async_computation | async-start | bytes 655360 | tf_op jit(solution)/shard_map/while/body/eval_jaxpr/all_to_all | solution.py:77
  427.4 16.3 %all-to-all-start.1 = ((bf16[32,2,2560]{2,1,0:T(2,128)(2,1)}), bf16[32,2,2560]{2,1,0:T(2,128)(2,1)S(1)}, u32[]{:S(2)}, u32[]{:S(2)}) async-start(bf16[32,2,2560]{2,1,0:T(2,128)(2,1)} %reshape.458), calls=%async_computation.1 | async-start | bytes 655360 | tf_op jit(solution)/shard_map/while/body/eval_jaxpr/all_to_all | solution.py:98
  447.0 6.9 collective-permute-start
  453.8 17.1 %copy-start.2 = (bf16[1,1,256,2560]{3,2,1,0:T(8,128)(2,1)S(1)}, bf16[1,1,256,2560]{3,2,1,0:T(8,128)(2,1)}, u32[]{:S(2)}) copy-start(bf16[1,1,256,2560]{3,2,1,0:T(8,128)(2,1)} %get-tuple-element.656) | copy-start | bytes 3932164 | tf_op jit(solution)/shard_map/while
  455.9 14.9 %all-to-all-start = ((bf16[32,2,2560]{2,1,0:T(2,128)(2,1)}), bf16[32,2,2560]{2,1,0:T(2,128)(2,1)S(1)}, u32[]{:S(2)}, u32[]{:S(2)}) async-start(bf16[32,2,2560]{2,1,0:T(2,128)(2,1)} %bitcast.136), calls=%async_computation | async-start | bytes 655360 | tf_op jit(solution)/shard_map/while/body/eval_jaxpr/all_to_all | solution.py:77
  478.5 15.1 %all-to-all-start.1 = ((bf16[32,2,2560]{2,1,0:T(2,128)(2,1)}), bf16[32,2,2560]{2,1,0:T(2,128)(2,1)S(1)}, u32[]{:S(2)}, u32[]{:S(2)}) async-start(bf16[32,2,2560]{2,1,0:T(2,128)(2,1)} %reshape.458), calls=%async_computation.1 | async-start | bytes 655360 | tf_op jit(solution)/shard_map/while/body/eval_jaxpr/all_to_all | solution.py:98
  496.8 6.6 collective-permute-start
  503.4 21.2 %copy-start.2 = (bf16[1,1,256,2560]{3,2,1,0:T(8,128)(2,1)S(1)}, bf16[1,1,256,2560]{3,2,1,0:T(8,128)(2,1)}, u32[]{:S(2)}) copy-start(bf16[1,1,256,2560]{3,2,1,0:T(8,128)(2,1)} %get-tuple-element.656) | copy-start | bytes 3932164 | tf_op jit(solution)/shard_map/while
  505.6 18.9 %all-to-all-start = ((bf16[32,2,2560]{2,1,0:T(2,128)(2,1)}), bf16[32,2,2560]{2,1,0:T(2,128)(2,1)S(1)}, u32[]{:S(2)}, u32[]{:S(2)}) async-start(bf16[32,2,2560]{2,1,0:T(2,128)(2,1)} %bitcast.136), calls=%async_computation | async-start | bytes 655360 | tf_op jit(solution)/shard_map/while/body/eval_jaxpr/all_to_all | solution.py:77
  532.2 15.1 %all-to-all-start.1 = ((bf16[32,2,2560]{2,1,0:T(2,128)(2,1)}), bf16[32,2,2560]{2,1,0:T(2,128)(2,1)S(1)}, u32[]{:S(2)}, u32[]{:S(2)}) async-start(bf16[32,2,2560]{2,1,0:T(2,128)(2,1)} %reshape.458), calls=%async_computation.1 | async-start | bytes 655360 | tf_op jit(solution)/shard_map/while/body/eval_jaxpr/all_to_all | solution.py:98
  550.5 6.7 collective-permute-start
  557.2 18.2 %copy-start.2 = (bf16[1,1,256,2560]{3,2,1,0:T(8,128)(2,1)S(1)}, bf16[1,1,256,2560]{3,2,1,0:T(8,128)(2,1)}, u32[]{:S(2)}) copy-start(bf16[1,1,256,2560]{3,2,1,0:T(8,128)(2,1)} %get-tuple-element.656) | copy-start | bytes 3932164 | tf_op jit(solution)/shard_map/while
  559.3 15.9 %all-to-all-start = ((bf16[32,2,2560]{2,1,0:T(2,128)(2,1)}), bf16[32,2,2560]{2,1,0:T(2,128)(2,1)S(1)}, u32[]{:S(2)}, u32[]{:S(2)}) async-start(bf16[32,2,2560]{2,1,0:T(2,128)(2,1)} %bitcast.136), calls=%async_computation | async-start | bytes 655360 | tf_op jit(solution)/shard_map/while/body/eval_jaxpr/all_to_all | solution.py:77
  582.9 15.9 %all-to-all-start.1 = ((bf16[32,2,2560]{2,1,0:T(2,128)(2,1)}), bf16[32,2,2560]{2,1,0:T(2,128)(2,1)S(1)}, u32[]{:S(2)}, u32[]{:S(2)}) async-start(bf16[32,2,2560]{2,1,0:T(2,128)(2,1)} %reshape.458), calls=%async_computation.1 | async-start | bytes 655360 | tf_op jit(solution)/shard_map/while/body/eval_jaxpr/all_to_all | solution.py:98
  602.1 6.4 collective-permute-start
  608.5 16.9 %copy-start.2 = (bf16[1,1,256,2560]{3,2,1,0:T(8,128)(2,1)S(1)}, bf16[1,1,256,2560]{3,2,1,0:T(8,128)(2,1)}, u32[]{:S(2)}) copy-start(bf16[1,1,256,2560]{3,2,1,0:T(8,128)(2,1)} %get-tuple-element.656) | copy-start | bytes 3932164 | tf_op jit(solution)/shard_map/while
  610.6 14.7 %all-to-all-start = ((bf16[32,2,2560]{2,1,0:T(2,128)(2,1)}), bf16[32,2,2560]{2,1,0:T(2,128)(2,1)S(1)}, u32[]{:S(2)}, u32[]{:S(2)}) async-start(bf16[32,2,2560]{2,1,0:T(2,128)(2,1)} %bitcast.136), calls=%async_computation | async-start | bytes 655360 | tf_op jit(solution)/shard_map/while/body/eval_jaxpr/all_to_all | solution.py:77
  632.9 14.7 %all-to-all-start.1 = ((bf16[32,2,2560]{2,1,0:T(2,128)(2,1)}), bf16[32,2,2560]{2,1,0:T(2,128)(2,1)S(1)}, u32[]{:S(2)}, u32[]{:S(2)}) async-start(bf16[32,2,2560]{2,1,0:T(2,128)(2,1)} %reshape.458), calls=%async_computation.1 | async-start | bytes 655360 | tf_op jit(solution)/shard_map/while/body/eval_jaxpr/all_to_all | solution.py:98
  650.9 6.8 collective-permute-start
  657.8 16.9 %copy-start.2 = (bf16[1,1,256,2560]{3,2,1,0:T(8,128)(2,1)S(1)}, bf16[1,1,256,2560]{3,2,1,0:T(8,128)(2,1)}, u32[]{:S(2)}) copy-start(bf16[1,1,256,2560]{3,2,1,0:T(8,128)(2,1)} %get-tuple-element.656) | copy-start | bytes 3932164 | tf_op jit(solution)/shard_map/while
  659.9 14.7 %all-to-all-start = ((bf16[32,2,2560]{2,1,0:T(2,128)(2,1)}), bf16[32,2,2560]{2,1,0:T(2,128)(2,1)S(1)}, u32[]{:S(2)}, u32[]{:S(2)}) async-start(bf16[32,2,2560]{2,1,0:T(2,128)(2,1)} %bitcast.136), calls=%async_computation | async-start | bytes 655360 | tf_op jit(solution)/shard_map/while/body/eval_jaxpr/all_to_all | solution.py:77
  682.2 14.7 %all-to-all-start.1 = ((bf16[32,2,2560]{2,1,0:T(2,128)(2,1)}), bf16[32,2,2560]{2,1,0:T(2,128)(2,1)S(1)}, u32[]{:S(2)}, u32[]{:S(2)}) async-start(bf16[32,2,2560]{2,1,0:T(2,128)(2,1)} %reshape.458), calls=%async_computation.1 | async-start | bytes 655360 | tf_op jit(solution)/shard_map/while/body/eval_jaxpr/all_to_all | solution.py:98
  700.2 6.5 collective-permute-start
  708.7 14.7 %all-to-all-start = ((bf16[32,2,2560]{2,1,0:T(2,128)(2,1)}), bf16[32,2,2560]{2,1,0:T(2,128)(2,1)S(1)}, u32[]{:S(2)}, u32[]{:S(2)}) async-start(bf16[32,2,2560]{2,1,0:T(2,128)(2,1)} %bitcast.136), calls=%async_computation | async-start | bytes 655360 | tf_op jit(solution)/shard_map/while/body/eval_jaxpr/all_to_all | solution.py:77
  731.1 14.7 %all-to-all-start.1 = ((bf16[32,2,2560]{2,1,0:T(2,128)(2,1)}), bf16[32,2,2560]{2,1,0:T(2,128)(2,1)S(1)}, u32[]{:S(2)}, u32[]{:S(2)}) async-start(bf16[32,2,2560]{2,1,0:T(2,128)(2,1)} %reshape.458), calls=%async_computation.1 | async-start | bytes 655360 | tf_op jit(solution)/shard_map/while/body/eval_jaxpr/all_to_all | solution.py:98
  749.0 6.5 collective-permute-start
  757.6 14.7 %all-to-all-start = ((bf16[32,2,2560]{2,1,0:T(2,128)(2,1)}), bf16[32,2,2560]{2,1,0:T(2,128)(2,1)S(1)}, u32[]{:S(2)}, u32[]{:S(2)}) async-start(bf16[32,2,2560]{2,1,0:T(2,128)(2,1)} %bitcast.136), calls=%async_computation | async-start | bytes 655360 | tf_op jit(solution)/shard_map/while/body/eval_jaxpr/all_to_all | solution.py:77
  780.0 14.7 %all-to-all-start.1 = ((bf16[32,2,2560]{2,1,0:T(2,128)(2,1)}), bf16[32,2,2560]{2,1,0:T(2,128)(2,1)S(1)}, u32[]{:S(2)}, u32[]{:S(2)}) async-start(bf16[32,2,2560]{2,1,0:T(2,128)(2,1)} %reshape.458), calls=%async_computation.1 | async-start | bytes 655360 | tf_op jit(solution)/shard_map/while/body/eval_jaxpr/all_to_all | solution.py:98
  798.0 6.3 collective-permute-start
  804.3 17.2 %copy-start.2 = (bf16[1,1,256,2560]{3,2,1,0:T(8,128)(2,1)S(1)}, bf16[1,1,256,2560]{3,2,1,0:T(8,128)(2,1)}, u32[]{:S(2)}) copy-start(bf16[1,1,256,2560]{3,2,1,0:T(8,128)(2,1)} %get-tuple-element.656) | copy-start | bytes 3932164 | tf_op jit(solution)/shard_map/while
  806.4 14.9 %all-to-all-start = ((bf16[32,2,2560]{2,1,0:T(2,128)(2,1)}), bf16[32,2,2560]{2,1,0:T(2,128)(2,1)S(1)}, u32[]{:S(2)}, u32[]{:S(2)}) async-start(bf16[32,2,2560]{2,1,0:T(2,128)(2,1)} %bitcast.136), calls=%async_computation | async-start | bytes 655360 | tf_op jit(solution)/shard_map/while/body/eval_jaxpr/all_to_all | solution.py:77
  829.0 15.8 %all-to-all-start.1 = ((bf16[32,2,2560]{2,1,0:T(2,128)(2,1)}), bf16[32,2,2560]{2,1,0:T(2,128)(2,1)S(1)}, u32[]{:S(2)}, u32[]{:S(2)}) async-start(bf16[32,2,2560]{2,1,0:T(2,128)(2,1)} %reshape.458), calls=%async_computation.1 | async-start | bytes 655360 | tf_op jit(solution)/shard_map/while/body/eval_jaxpr/all_to_all | solution.py:98
  848.1 7.1 collective-permute-start
  859.1 88.6 %reduce-scatter.3.cloned.1.call-start = ((), (), s32[]{:S(2)}) async-start(), calls=%async_computation.8 | async-start | bytes 1966080 | tf_op jit(solution)/shard_map/reduce_scatter | solution.py:148
  (38 other events, 273.3 us)
Sparse Core Ops, SparseCore 0:
  30.2 23.7 all-gather.3
  56.1 18.8 all-gather.5
  77.0 18.8 all-gather.7
  859.2 67.0 reduce-scatter.4
  929.5 18.1 reduce-scatter.2
where the time goes:
time: 959 us; the launch traced here: 954 us
  waiting for transfers between devices  511 us (53%)
  starting transfers between devices  159 us (17%)
  matrix products  123 us (13%)
  local copies, waits for them, and re-layouts  62.3 us (6%)
  other arithmetic  55 us (6%)
  blocking collectives  28.2 us (3%)
  between operations  13.9 us (1%)
    all_to_all x15, waiting for transfers between devices, tick_step(): lax.all_to_all(partial_value.reshape(width_all, capacity, feature_count),...  164 us
    all_to_all x15, waiting for transfers between devices, tick_step(): lax.all_to_all(sending, 'expert', split_axis=0, concat_axis=0, tiled=True)  156 us
    ppermute x15, waiting for transfers between devices, shifted(): return lax.ppermute(block, axis, route)  77.9 us
    all_to_all x15, starting transfers between devices, tick_step(): lax.all_to_all(sending, 'expert', split_axis=0, concat_axis=0, tiled=True)  66.2 us
    reduce_scatter x1, waiting for transfers between devices, shards(): lax.psum_scatter(part_up.astype(jnp.bfloat16), 'dp', scatter_dimension=2,...  64.3 us
    all_to_all x15, starting transfers between devices, tick_step(): lax.all_to_all(partial_value.reshape(width_all, capacity, feature_count),...  62.6 us
    dot_general x15, matrix products, tick_step(): jnp.einsum('rd,hd->rh', unit_now, gate_slab, preferred_element_type=jnp.f...  41.8 us
    dot_general x15, matrix products, tick_step(): jnp.einsum('rd,hd->rh', unit_now, up_slab, preferred_element_type=jnp.flo...  40 us
  transfers between devices with their start and end apart: 51, of which 48 were waited for; matrix products, arithmetic and copies ran while one was open for 3% of the time, Pallas kernels for 0%

commit v1 on v0

--- a/solution.py
+++ b/solution.py
@@ -56,7 +56,12 @@
         stretches, MICRO, experts, capacity, feature_count
     )
     unit_send = jnp.repeat(unit_slots, GROUP, axis=2)
-    unit_recv = lax.all_to_all(unit_send, "expert", split_axis=2, concat_axis=2, tiled=True)
+    unit_recv = jnp.concatenate(
+        lax.all_to_all(
+            jnp.stack(jnp.split(unit_send, lax.axis_size("expert"), axis=2)), "expert", 0, 0
+        ),
+        axis=2,
+    )
     unit_rows = unit_recv.reshape(stretches, MICRO, slot_count, feature_count)
     top_section = section_index == sections - 1
 

time: 959 us -> 989 us (1.031)
  local copies, waits for them, and re-layouts: 62.3 us -> 82.8 us
    unnamed x13 -> x42, local copies, waits for them, and re-layouts: 1.44 us -> 21.8 us
    dot_general x15, matrix products: 7.67 us -> 27.4 us  [tick_step(): jnp.einsum('rd,hd->rh', grad_rows, down_slab, preferred_element_type=jnp....]
    dot_general x15, matrix products: 17.1 us -> 2.3 us  [tick_step(): jnp.einsum('ect,td->ecd', place_now, grad_in, preferred_element_type=jnp....]
where the time goes in v1:
time: 989 us; the launch traced here: 984 us
  waiting for transfers between devices  516 us (52%)
  starting transfers between devices  160 us (16%)
  matrix products  127 us (13%)
  local copies, waits for them, and re-layouts  82.8 us (8%)
  other arithmetic  53 us (5%)
  blocking collectives  28.9 us (3%)
  between operations  13.9 us (1%)
    all_to_all x15, waiting for transfers between devices, tick_step(): lax.all_to_all(partial_value.reshape(width_all, capacity, feature_count),...  164 us
    all_to_all x15, waiting for transfers between devices, tick_step(): lax.all_to_all(sending, 'expert', split_axis=0, concat_axis=0, tiled=True)  157 us
    ppermute x15, waiting for transfers between devices, shifted(): return lax.ppermute(block, axis, route)  76.5 us
    reduce_scatter x1, waiting for transfers between devices, shards(): lax.psum_scatter(part_up.astype(jnp.bfloat16), 'dp', scatter_dimension=2,...  68 us
    all_to_all x15, starting transfers between devices, tick_step(): lax.all_to_all(sending, 'expert', split_axis=0, concat_axis=0, tiled=True)  67.7 us
    all_to_all x15, starting transfers between devices, tick_step(): lax.all_to_all(partial_value.reshape(width_all, capacity, feature_count),...  62 us
    dot_general x15, matrix products, tick_step(): jnp.einsum('rd,hd->rh', unit_now, gate_slab, preferred_element_type=jnp.f...  40.3 us
    dot_general x15, matrix products, tick_step(): jnp.einsum('rd,hd->rh', unit_now, up_slab, preferred_element_type=jnp.flo...  40.1 us
  transfers between devices with their start and end apart: 51, of which 48 were waited for; matrix products, arithmetic and copies ran while one was open for 3% of the time, Pallas kernels for 0%

profile of v1, /device:TPU:1, one launch (start us, length us, event | category | flops | bytes accessed | tf_op | source)
XLA Modules:
  0.0 983.7 jit_solution(10738537261919837827)
XLA Ops:
  37.1 10.7 %all-to-all-start.2 = ((bf16[32,1,8,1,2,2560]{5,4,2,3,1,0:T(2,128)(2,1)}), bf16[32,1,8,1,2,2560]{5,4,2,3,1,0:T(2,128)(2,1)}, u32[]{:S(2)}, u32[]{:S(2)}) async-start(bf16[32,1,8,1,2,2560]{5,4,2,3,1,0:T(2,128)(2,1)} %fusion.45), calls=%async_computation.2 | async-start | bytes 5242880 | tf_op jit(solution)/shard_map/all_to_all | solution.py:60
  50.1 28.9 %all_gather.12 = bf16[128,2560]{0,1:T(8,128)(2,1)S(1)} all-gather(bf16[128,320]{0,1:T(8,128)(2,1)S(1)} %copy-done.6), channel_id=1, replica_groups=mesh['pipe'=8,'expert'=32,'dp'=2] {'pipe'}, dimensions={1}, use_global_device_ids=true | all-gather | bytes 737280 | tf_op jit(solution)/shard_map/all_gather | solution.py:37
  80.7 26.8 %all-to-all-done.2 = bf16[32,1,8,1,2,2560]{5,4,2,3,1,0:T(2,128)(2,1)} async-done(((bf16[32,1,8,1,2,2560]{5,4,2,3,1,0:T(2,128)(2,1)}), bf16[32,1,8,1,2,2560]{5,4,2,3,1,0:T(2,128)(2,1)}, u32[]{:S(2)}, u32[]{:S(2)}) %all-to-all-start.2) | async-done | bytes 2621472 | tf_op jit(solution)/shard_map/all_to_all | solution.py:60
  113.2 6.7 reshape.422
  123.6 758.2 %while.21 = (s32[]{:T(128)}, bf16[16,2560]{1,0:T(8,128)(2,1)S(1)}, bf16[1,8,64,256]{3,2,1,0:T(8,128)(2,1)}, bf16[1,8,64,256]{3,2,1,0:T(8,128)(2,1)}, s32[]{:T(12...) while((s32[]{:T(128)}, bf16[16,2560]{1,0:T(8,128)(2,1)S(1)}, ...), condition=%wide.region_7.8_spmd, body=%wide.region_3.7_spmd.sunk | while | flops 422298752 | bytes 31978876 | solution.py:138
  124.9 6.8 all-to-all-start
  132.4 10.5 %all-to-all-done = bf16[32,2,2560]{2,1,0:T(2,128)(2,1)S(1)} async-done(((bf16[32,2,2560]{2,1,0:T(2,128)(2,1)}), bf16[32,2,2560]{2,1,0:T(2,128)(2,1)S(1)}, u32[]{:S(2)}, u32[]{:S(2)}) %all-to-all-start) | async-done | bytes 327712 | tf_op jit(solution)/shard_map/while/body/eval_jaxpr/all_to_all | solution.py:82
  151.8 5.9 all-to-all-start.1
  157.8 10.7 %all-to-all-done.1 = bf16[32,2,2560]{2,1,0:T(2,128)(2,1)S(1)} async-done(((bf16[32,2,2560]{2,1,0:T(2,128)(2,1)}), bf16[32,2,2560]{2,1,0:T(2,128)(2,1)S(1)}, u32[]{:S(2)}, u32[]{:S(2)}) %all-to-all-start.1) | async-done | bytes 327712 | tf_op jit(solution)/shard_map/while/body/eval_jaxpr/all_to_all | solution.py:103
  173.0 4.5 collective-permute-done
  178.6 6.4 all-to-all-start
  185.7 10.1 %all-to-all-done = bf16[32,2,2560]{2,1,0:T(2,128)(2,1)S(1)} async-done(((bf16[32,2,2560]{2,1,0:T(2,128)(2,1)}), bf16[32,2,2560]{2,1,0:T(2,128)(2,1)S(1)}, u32[]{:S(2)}, u32[]{:S(2)}) %all-to-all-start) | async-done | bytes 327712 | tf_op jit(solution)/shard_map/while/body/eval_jaxpr/all_to_all | solution.py:82
  204.8 4.3 all-to-all-start.1
  209.1 10.7 %all-to-all-done.1 = bf16[32,2,2560]{2,1,0:T(2,128)(2,1)S(1)} async-done(((bf16[32,2,2560]{2,1,0:T(2,128)(2,1)}), bf16[32,2,2560]{2,1,0:T(2,128)(2,1)S(1)}, u32[]{:S(2)}, u32[]{:S(2)}) %all-to-all-start.1) | async-done | bytes 327712 | tf_op jit(solution)/shard_map/while/body/eval_jaxpr/all_to_all | solution.py:103
  224.4 4.6 collective-permute-done
  230.1 4.3 all-to-all-start
  235.1 10.0 %all-to-all-done = bf16[32,2,2560]{2,1,0:T(2,128)(2,1)S(1)} async-done(((bf16[32,2,2560]{2,1,0:T(2,128)(2,1)}), bf16[32,2,2560]{2,1,0:T(2,128)(2,1)S(1)}, u32[]{:S(2)}, u32[]{:S(2)}) %all-to-all-start) | async-done | bytes 327712 | tf_op jit(solution)/shard_map/while/body/eval_jaxpr/all_to_all | solution.py:82
  258.1 10.6 %all-to-all-done.1 = bf16[32,2,2560]{2,1,0:T(2,128)(2,1)S(1)} async-done(((bf16[32,2,2560]{2,1,0:T(2,128)(2,1)}), bf16[32,2,2560]{2,1,0:T(2,128)(2,1)S(1)}, u32[]{:S(2)}, u32[]{:S(2)}) %all-to-all-start.1) | async-done | bytes 327712 | tf_op jit(solution)/shard_map/while/body/eval_jaxpr/all_to_all | solution.py:103
  273.3 4.5 collective-permute-done
  279.0 4.1 all-to-all-start
  283.8 10.0 %all-to-all-done = bf16[32,2,2560]{2,1,0:T(2,128)(2,1)S(1)} async-done(((bf16[32,2,2560]{2,1,0:T(2,128)(2,1)}), bf16[32,2,2560]{2,1,0:T(2,128)(2,1)S(1)}, u32[]{:S(2)}, u32[]{:S(2)}) %all-to-all-start) | async-done | bytes 327712 | tf_op jit(solution)/shard_map/while/body/eval_jaxpr/all_to_all | solution.py:82
  306.7 10.6 %all-to-all-done.1 = bf16[32,2,2560]{2,1,0:T(2,128)(2,1)S(1)} async-done(((bf16[32,2,2560]{2,1,0:T(2,128)(2,1)}), bf16[32,2,2560]{2,1,0:T(2,128)(2,1)S(1)}, u32[]{:S(2)}, u32[]{:S(2)}) %all-to-all-start.1) | async-done | bytes 327712 | tf_op jit(solution)/shard_map/while/body/eval_jaxpr/all_to_all | solution.py:103
  321.9 6.0 collective-permute-done
  329.0 4.1 all-to-all-start
  333.8 10.0 %all-to-all-done = bf16[32,2,2560]{2,1,0:T(2,128)(2,1)S(1)} async-done(((bf16[32,2,2560]{2,1,0:T(2,128)(2,1)}), bf16[32,2,2560]{2,1,0:T(2,128)(2,1)S(1)}, u32[]{:S(2)}, u32[]{:S(2)}) %all-to-all-start) | async-done | bytes 327712 | tf_op jit(solution)/shard_map/while/body/eval_jaxpr/all_to_all | solution.py:82
  356.8 10.6 %all-to-all-done.1 = bf16[32,2,2560]{2,1,0:T(2,128)(2,1)S(1)} async-done(((bf16[32,2,2560]{2,1,0:T(2,128)(2,1)}), bf16[32,2,2560]{2,1,0:T(2,128)(2,1)S(1)}, u32[]{:S(2)}, u32[]{:S(2)}) %all-to-all-start.1) | async-done | bytes 327712 | tf_op jit(solution)/shard_map/while/body/eval_jaxpr/all_to_all | solution.py:103
  371.9 5.4 collective-permute-done
  378.5 4.1 all-to-all-start
  383.3 10.0 %all-to-all-done = bf16[32,2,2560]{2,1,0:T(2,128)(2,1)S(1)} async-done(((bf16[32,2,2560]{2,1,0:T(2,128)(2,1)}), bf16[32,2,2560]{2,1,0:T(2,128)(2,1)S(1)}, u32[]{:S(2)}, u32[]{:S(2)}) %all-to-all-start) | async-done | bytes 327712 | tf_op jit(solution)/shard_map/while/body/eval_jaxpr/all_to_all | solution.py:82
  406.2 10.6 %all-to-all-done.1 = bf16[32,2,2560]{2,1,0:T(2,128)(2,1)S(1)} async-done(((bf16[32,2,2560]{2,1,0:T(2,128)(2,1)}), bf16[32,2,2560]{2,1,0:T(2,128)(2,1)S(1)}, u32[]{:S(2)}, u32[]{:S(2)}) %all-to-all-start.1) | async-done | bytes 327712 | tf_op jit(solution)/shard_map/while/body/eval_jaxpr/all_to_all | solution.py:103
  421.4 5.1 collective-permute-done
  427.6 4.1 all-to-all-start
  432.4 10.0 %all-to-all-done = bf16[32,2,2560]{2,1,0:T(2,128)(2,1)S(1)} async-done(((bf16[32,2,2560]{2,1,0:T(2,128)(2,1)}), bf16[32,2,2560]{2,1,0:T(2,128)(2,1)S(1)}, u32[]{:S(2)}, u32[]{:S(2)}) %all-to-all-start) | async-done | bytes 327712 | tf_op jit(solution)/shard_map/while/body/eval_jaxpr/all_to_all | solution.py:82
  455.3 12.1 %all-to-all-done.1 = bf16[32,2,2560]{2,1,0:T(2,128)(2,1)S(1)} async-done(((bf16[32,2,2560]{2,1,0:T(2,128)(2,1)}), bf16[32,2,2560]{2,1,0:T(2,128)(2,1)S(1)}, u32[]{:S(2)}, u32[]{:S(2)}) %all-to-all-start.1) | async-done | bytes 327712 | tf_op jit(solution)/shard_map/while/body/eval_jaxpr/all_to_all | solution.py:103
  471.9 5.1 collective-permute-done
  482.9 11.5 %all-to-all-done = bf16[32,2,2560]{2,1,0:T(2,128)(2,1)S(1)} async-done(((bf16[32,2,2560]{2,1,0:T(2,128)(2,1)}), bf16[32,2,2560]{2,1,0:T(2,128)(2,1)S(1)}, u32[]{:S(2)}, u32[]{:S(2)}) %all-to-all-start) | async-done | bytes 327712 | tf_op jit(solution)/shard_map/while/body/eval_jaxpr/all_to_all | solution.py:82
  507.3 11.1 %all-to-all-done.1 = bf16[32,2,2560]{2,1,0:T(2,128)(2,1)S(1)} async-done(((bf16[32,2,2560]{2,1,0:T(2,128)(2,1)}), bf16[32,2,2560]{2,1,0:T(2,128)(2,1)S(1)}, u32[]{:S(2)}, u32[]{:S(2)}) %all-to-all-start.1) | async-done | bytes 327712 | tf_op jit(solution)/shard_map/while/body/eval_jaxpr/all_to_all | solution.py:103
  522.9 6.8 collective-permute-done
  530.9 4.9 all-to-all-start
  536.5 13.3 %all-to-all-done = bf16[32,2,2560]{2,1,0:T(2,128)(2,1)S(1)} async-done(((bf16[32,2,2560]{2,1,0:T(2,128)(2,1)}), bf16[32,2,2560]{2,1,0:T(2,128)(2,1)S(1)}, u32[]{:S(2)}, u32[]{:S(2)}) %all-to-all-start) | async-done | bytes 327712 | tf_op jit(solution)/shard_map/while/body/eval_jaxpr/all_to_all | solution.py:82
  558.7 4.5 all-to-all-start.1
  563.3 10.8 %all-to-all-done.1 = bf16[32,2,2560]{2,1,0:T(2,128)(2,1)S(1)} async-done(((bf16[32,2,2560]{2,1,0:T(2,128)(2,1)}), bf16[32,2,2560]{2,1,0:T(2,128)(2,1)S(1)}, u32[]{:S(2)}, u32[]{:S(2)}) %all-to-all-start.1) | async-done | bytes 327712 | tf_op jit(solution)/shard_map/while/body/eval_jaxpr/all_to_all | solution.py:103
  583.6 4.7 all-to-all-start
  589.1 10.1 %all-to-all-done = bf16[32,2,2560]{2,1,0:T(2,128)(2,1)S(1)} async-done(((bf16[32,2,2560]{2,1,0:T(2,128)(2,1)}), bf16[32,2,2560]{2,1,0:T(2,128)(2,1)S(1)}, u32[]{:S(2)}, u32[]{:S(2)}) %all-to-all-start) | async-done | bytes 327712 | tf_op jit(solution)/shard_map/while/body/eval_jaxpr/all_to_all | solution.py:82
  608.1 4.1 all-to-all-start.1
  612.3 10.7 %all-to-all-done.1 = bf16[32,2,2560]{2,1,0:T(2,128)(2,1)S(1)} async-done(((bf16[32,2,2560]{2,1,0:T(2,128)(2,1)}), bf16[32,2,2560]{2,1,0:T(2,128)(2,1)S(1)}, u32[]{:S(2)}, u32[]{:S(2)}) %all-to-all-start.1) | async-done | bytes 327712 | tf_op jit(solution)/shard_map/while/body/eval_jaxpr/all_to_all | solution.py:103
  632.5 4.1 all-to-all-start
  637.3 10.0 %all-to-all-done = bf16[32,2,2560]{2,1,0:T(2,128)(2,1)S(1)} async-done(((bf16[32,2,2560]{2,1,0:T(2,128)(2,1)}), bf16[32,2,2560]{2,1,0:T(2,128)(2,1)S(1)}, u32[]{:S(2)}, u32[]{:S(2)}) %all-to-all-start) | async-done | bytes 327712 | tf_op jit(solution)/shard_map/while/body/eval_jaxpr/all_to_all | solution.py:82
  660.3 10.6 %all-to-all-done.1 = bf16[32,2,2560]{2,1,0:T(2,128)(2,1)S(1)} async-done(((bf16[32,2,2560]{2,1,0:T(2,128)(2,1)}), bf16[32,2,2560]{2,1,0:T(2,128)(2,1)S(1)}, u32[]{:S(2)}, u32[]{:S(2)}) %all-to-all-start.1) | async-done | bytes 327712 | tf_op jit(solution)/shard_map/while/body/eval_jaxpr/all_to_all | solution.py:103
  675.4 4.7 collective-permute-done
  686.1 10.0 %all-to-all-done = bf16[32,2,2560]{2,1,0:T(2,128)(2,1)S(1)} async-done(((bf16[32,2,2560]{2,1,0:T(2,128)(2,1)}), bf16[32,2,2560]{2,1,0:T(2,128)(2,1)S(1)}, u32[]{:S(2)}, u32[]{:S(2)}) %all-to-all-start) | async-done | bytes 327712 | tf_op jit(solution)/shard_map/while/body/eval_jaxpr/all_to_all | solution.py:82
  709.0 10.6 %all-to-all-done.1 = bf16[32,2,2560]{2,1,0:T(2,128)(2,1)S(1)} async-done(((bf16[32,2,2560]{2,1,0:T(2,128)(2,1)}), bf16[32,2,2560]{2,1,0:T(2,128)(2,1)S(1)}, u32[]{:S(2)}, u32[]{:S(2)}) %all-to-all-start.1) | async-done | bytes 327712 | tf_op jit(solution)/shard_map/while/body/eval_jaxpr/all_to_all | solution.py:103
  724.2 7.0 collective-permute-done
  737.0 10.5 %all-to-all-done = bf16[32,2,2560]{2,1,0:T(2,128)(2,1)S(1)} async-done(((bf16[32,2,2560]{2,1,0:T(2,128)(2,1)}), bf16[32,2,2560]{2,1,0:T(2,128)(2,1)S(1)}, u32[]{:S(2)}, u32[]{:S(2)}) %all-to-all-start) | async-done | bytes 327712 | tf_op jit(solution)/shard_map/while/body/eval_jaxpr/all_to_all | solution.py:82
  760.3 11.1 %all-to-all-done.1 = bf16[32,2,2560]{2,1,0:T(2,128)(2,1)S(1)} async-done(((bf16[32,2,2560]{2,1,0:T(2,128)(2,1)}), bf16[32,2,2560]{2,1,0:T(2,128)(2,1)S(1)}, u32[]{:S(2)}, u32[]{:S(2)}) %all-to-all-start.1) | async-done | bytes 327712 | tf_op jit(solution)/shard_map/while/body/eval_jaxpr/all_to_all | solution.py:103
  775.9 5.5 collective-permute-done
  787.3 10.5 %all-to-all-done = bf16[32,2,2560]{2,1,0:T(2,128)(2,1)S(1)} async-done(((bf16[32,2,2560]{2,1,0:T(2,128)(2,1)}), bf16[32,2,2560]{2,1,0:T(2,128)(2,1)S(1)}, u32[]{:S(2)}, u32[]{:S(2)}) %all-to-all-start) | async-done | bytes 327712 | tf_op jit(solution)/shard_map/while/body/eval_jaxpr/all_to_all | solution.py:82
  810.6 11.1 %all-to-all-done.1 = bf16[32,2,2560]{2,1,0:T(2,128)(2,1)S(1)} async-done(((bf16[32,2,2560]{2,1,0:T(2,128)(2,1)}), bf16[32,2,2560]{2,1,0:T(2,128)(2,1)S(1)}, u32[]{:S(2)}, u32[]{:S(2)}) %all-to-all-start.1) | async-done | bytes 327712 | tf_op jit(solution)/shard_map/while/body/eval_jaxpr/all_to_all | solution.py:103
  826.2 4.3 collective-permute-done
  836.4 10.4 %all-to-all-done = bf16[32,2,2560]{2,1,0:T(2,128)(2,1)S(1)} async-done(((bf16[32,2,2560]{2,1,0:T(2,128)(2,1)}), bf16[32,2,2560]{2,1,0:T(2,128)(2,1)S(1)}, u32[]{:S(2)}, u32[]{:S(2)}) %all-to-all-start) | async-done | bytes 327712 | tf_op jit(solution)/shard_map/while/body/eval_jaxpr/all_to_all | solution.py:82
  859.7 12.3 %all-to-all-done.1 = bf16[32,2,2560]{2,1,0:T(2,128)(2,1)S(1)} async-done(((bf16[32,2,2560]{2,1,0:T(2,128)(2,1)}), bf16[32,2,2560]{2,1,0:T(2,128)(2,1)S(1)}, u32[]{:S(2)}, u32[]{:S(2)}) %all-to-all-start.1) | async-done | bytes 327712 | tf_op jit(solution)/shard_map/while/body/eval_jaxpr/all_to_all | solution.py:103
  876.5 5.3 collective-permute-done
  887.7 68.0 %reduce-scatter.5.cloned.1.call-done = bf16[1,256,1280]{2,1,0:T(8,128)(2,1)} async-done(((bf16[1,256,2560]{2,1,0:T(8,128)(2,1)}), bf16[1,256,1280]{2,1,0:T(8,128)(2,1)}) %reduce-scatter.5.cloned.1.call-update) | async-done | bytes 655376 | tf_op jit(solution)/shard_map/reduce_scatter | solution.py:156
  955.8 21.4 %reduce-scatter.3.cloned.1.call-done = bf16[1,256,1280]{2,1,0:T(8,128)(2,1)} async-done(((bf16[1,256,2560]{2,1,0:T(8,128)(2,1)}), bf16[1,256,1280]{2,1,0:T(8,128)(2,1)}) %reduce-scatter.3.cloned.1.call-update) | async-done | bytes 655376 | tf_op jit(solution)/shard_map/reduce_scatter | solution.py:153
  (567 shorter events, 348.9 us)
Async XLA Ops:
  37.1 70.4 %all-to-all-start.2 = ((bf16[32,1,8,1,2,2560]{5,4,2,3,1,0:T(2,128)(2,1)}), bf16[32,1,8,1,2,2560]{5,4,2,3,1,0:T(2,128)(2,1)}, u32[]{:S(2)}, u32[]{:S(2)}) async-start(bf16[32,1,8,1,2,2560]{5,4,2,3,1,0:T(2,128)(2,1)} %fusion.45), calls=%async_computation.2 | async-start | bytes 5242880 | tf_op jit(solution)/shard_map/all_to_all | solution.py:60
  47.9 74.3 %all-gather.4.cloned.1.call-start = ((), (), s32[]{:S(2)}) async-start(), calls=%async_computation.5 | async-start | bytes 1966080 | tf_op jit(solution)/shard_map/all_gather | solution.py:42
  48.6 73.6 %all-gather.6.cloned.1.call-start = ((), (), s32[]{:S(2)}) async-start(), calls=%async_computation.6 | async-start | bytes 1966080 | tf_op jit(solution)/shard_map/all_gather | solution.py:41
  49.4 72.8 %all-gather.8.cloned.1.call-start = ((), (), s32[]{:S(2)}) async-start(), calls=%async_computation.7 | async-start | bytes 1966080 | tf_op jit(solution)/shard_map/all_gather | solution.py:40
  50.1 905.7 %reduce-scatter.5.cloned.1.call-start = ((), (), s32[]{:S(2)}) async-start(), calls=%async_computation.9 | async-start | bytes 1966080 | tf_op jit(solution)/shard_map/reduce_scatter | solution.py:156
  123.7 21.2 %copy-start.1 = (bf16[1,1,256,2560]{3,2,1,0:T(8,128)(2,1)S(1)}, bf16[1,1,256,2560]{3,2,1,0:T(8,128)(2,1)}, u32[]{:S(2)}) copy-start(bf16[1,1,256,2560]{3,2,1,0:T(8,128)(2,1)} %get-tuple-element.661) | copy-start | bytes 3932164 | tf_op jit(solution)/shard_map/while
  123.9 23.6 %copy-start = (bf16[1,1,256,2560]{3,2,1,0:T(8,128)(2,1)S(1)}, bf16[1,1,256,2560]{3,2,1,0:T(8,128)(2,1)}, u32[]{:S(2)}) copy-start(bf16[1,1,256,2560]{3,2,1,0:T(8,128)(2,1)} %get-tuple-element.660) | copy-start | bytes 3932164 | tf_op jit(solution)/shard_map/while
  124.9 18.0 %all-to-all-start = ((bf16[32,2,2560]{2,1,0:T(2,128)(2,1)}), bf16[32,2,2560]{2,1,0:T(2,128)(2,1)S(1)}, u32[]{:S(2)}, u32[]{:S(2)}) async-start(bf16[32,2,2560]{2,1,0:T(2,128)(2,1)} %bitcast.270), calls=%async_computation | async-start | bytes 655360 | tf_op jit(solution)/shard_map/while/body/eval_jaxpr/all_to_all | solution.py:82
  151.8 16.7 %all-to-all-start.1 = ((bf16[32,2,2560]{2,1,0:T(2,128)(2,1)}), bf16[32,2,2560]{2,1,0:T(2,128)(2,1)S(1)}, u32[]{:S(2)}, u32[]{:S(2)}) async-start(bf16[32,2,2560]{2,1,0:T(2,128)(2,1)} %reshape.458), calls=%async_computation.1 | async-start | bytes 655360 | tf_op jit(solution)/shard_map/while/body/eval_jaxpr/all_to_all | solution.py:103
  171.7 5.8 collective-permute-start
  177.7 22.8 %copy-start = (bf16[1,1,256,2560]{3,2,1,0:T(8,128)(2,1)S(1)}, bf16[1,1,256,2560]{3,2,1,0:T(8,128)(2,1)}, u32[]{:S(2)}) copy-start(bf16[1,1,256,2560]{3,2,1,0:T(8,128)(2,1)} %get-tuple-element.660) | copy-start | bytes 3932164 | tf_op jit(solution)/shard_map/while
  178.6 17.2 %all-to-all-start = ((bf16[32,2,2560]{2,1,0:T(2,128)(2,1)}), bf16[32,2,2560]{2,1,0:T(2,128)(2,1)S(1)}, u32[]{:S(2)}, u32[]{:S(2)}) async-start(bf16[32,2,2560]{2,1,0:T(2,128)(2,1)} %bitcast.270), calls=%async_computation | async-start | bytes 655360 | tf_op jit(solution)/shard_map/while/body/eval_jaxpr/all_to_all | solution.py:82
  204.8 15.1 %all-to-all-start.1 = ((bf16[32,2,2560]{2,1,0:T(2,128)(2,1)}), bf16[32,2,2560]{2,1,0:T(2,128)(2,1)S(1)}, u32[]{:S(2)}, u32[]{:S(2)}) async-start(bf16[32,2,2560]{2,1,0:T(2,128)(2,1)} %reshape.458), calls=%async_computation.1 | async-start | bytes 655360 | tf_op jit(solution)/shard_map/while/body/eval_jaxpr/all_to_all | solution.py:103
  223.1 5.9 collective-permute-start
  229.2 20.6 %copy-start = (bf16[1,1,256,2560]{3,2,1,0:T(8,128)(2,1)S(1)}, bf16[1,1,256,2560]{3,2,1,0:T(8,128)(2,1)}, u32[]{:S(2)}) copy-start(bf16[1,1,256,2560]{3,2,1,0:T(8,128)(2,1)} %get-tuple-element.660) | copy-start | bytes 3932164 | tf_op jit(solution)/shard_map/while
  230.1 15.1 %all-to-all-start = ((bf16[32,2,2560]{2,1,0:T(2,128)(2,1)}), bf16[32,2,2560]{2,1,0:T(2,128)(2,1)S(1)}, u32[]{:S(2)}, u32[]{:S(2)}) async-start(bf16[32,2,2560]{2,1,0:T(2,128)(2,1)} %bitcast.270), calls=%async_computation | async-start | bytes 655360 | tf_op jit(solution)/shard_map/while/body/eval_jaxpr/all_to_all | solution.py:82
  254.0 14.7 %all-to-all-start.1 = ((bf16[32,2,2560]{2,1,0:T(2,128)(2,1)}), bf16[32,2,2560]{2,1,0:T(2,128)(2,1)S(1)}, u32[]{:S(2)}, u32[]{:S(2)}) async-start(bf16[32,2,2560]{2,1,0:T(2,128)(2,1)} %reshape.458), calls=%async_computation.1 | async-start | bytes 655360 | tf_op jit(solution)/shard_map/while/body/eval_jaxpr/all_to_all | solution.py:103
  272.0 5.8 collective-permute-start
  279.0 14.8 %all-to-all-start = ((bf16[32,2,2560]{2,1,0:T(2,128)(2,1)}), bf16[32,2,2560]{2,1,0:T(2,128)(2,1)S(1)}, u32[]{:S(2)}, u32[]{:S(2)}) async-start(bf16[32,2,2560]{2,1,0:T(2,128)(2,1)} %bitcast.270), calls=%async_computation | async-start | bytes 655360 | tf_op jit(solution)/shard_map/while/body/eval_jaxpr/all_to_all | solution.py:82
  302.7 14.7 %all-to-all-start.1 = ((bf16[32,2,2560]{2,1,0:T(2,128)(2,1)}), bf16[32,2,2560]{2,1,0:T(2,128)(2,1)S(1)}, u32[]{:S(2)}, u32[]{:S(2)}) async-start(bf16[32,2,2560]{2,1,0:T(2,128)(2,1)} %reshape.458), calls=%async_computation.1 | async-start | bytes 655360 | tf_op jit(solution)/shard_map/while/body/eval_jaxpr/all_to_all | solution.py:103
  320.6 7.3 collective-permute-start
  328.1 20.4 %copy-start = (bf16[1,1,256,2560]{3,2,1,0:T(8,128)(2,1)S(1)}, bf16[1,1,256,2560]{3,2,1,0:T(8,128)(2,1)}, u32[]{:S(2)}) copy-start(bf16[1,1,256,2560]{3,2,1,0:T(8,128)(2,1)} %get-tuple-element.660) | copy-start | bytes 3932164 | tf_op jit(solution)/shard_map/while
  329.0 14.8 %all-to-all-start = ((bf16[32,2,2560]{2,1,0:T(2,128)(2,1)}), bf16[32,2,2560]{2,1,0:T(2,128)(2,1)S(1)}, u32[]{:S(2)}, u32[]{:S(2)}) async-start(bf16[32,2,2560]{2,1,0:T(2,128)(2,1)} %bitcast.270), calls=%async_computation | async-start | bytes 655360 | tf_op jit(solution)/shard_map/while/body/eval_jaxpr/all_to_all | solution.py:82
  352.7 14.7 %all-to-all-start.1 = ((bf16[32,2,2560]{2,1,0:T(2,128)(2,1)}), bf16[32,2,2560]{2,1,0:T(2,128)(2,1)S(1)}, u32[]{:S(2)}, u32[]{:S(2)}) async-start(bf16[32,2,2560]{2,1,0:T(2,128)(2,1)} %reshape.458), calls=%async_computation.1 | async-start | bytes 655360 | tf_op jit(solution)/shard_map/while/body/eval_jaxpr/all_to_all | solution.py:103
  370.6 6.7 collective-permute-start
  378.5 14.8 %all-to-all-start = ((bf16[32,2,2560]{2,1,0:T(2,128)(2,1)}), bf16[32,2,2560]{2,1,0:T(2,128)(2,1)S(1)}, u32[]{:S(2)}, u32[]{:S(2)}) async-start(bf16[32,2,2560]{2,1,0:T(2,128)(2,1)} %bitcast.270), calls=%async_computation | async-start | bytes 655360 | tf_op jit(solution)/shard_map/while/body/eval_jaxpr/all_to_all | solution.py:82
  402.2 14.7 %all-to-all-start.1 = ((bf16[32,2,2560]{2,1,0:T(2,128)(2,1)}), bf16[32,2,2560]{2,1,0:T(2,128)(2,1)S(1)}, u32[]{:S(2)}, u32[]{:S(2)}) async-start(bf16[32,2,2560]{2,1,0:T(2,128)(2,1)} %reshape.458), calls=%async_computation.1 | async-start | bytes 655360 | tf_op jit(solution)/shard_map/while/body/eval_jaxpr/all_to_all | solution.py:103
  420.1 6.4 collective-permute-start
  427.6 14.8 %all-to-all-start = ((bf16[32,2,2560]{2,1,0:T(2,128)(2,1)}), bf16[32,2,2560]{2,1,0:T(2,128)(2,1)S(1)}, u32[]{:S(2)}, u32[]{:S(2)}) async-start(bf16[32,2,2560]{2,1,0:T(2,128)(2,1)} %bitcast.270), calls=%async_computation | async-start | bytes 655360 | tf_op jit(solution)/shard_map/while/body/eval_jaxpr/all_to_all | solution.py:82
  451.3 16.1 %all-to-all-start.1 = ((bf16[32,2,2560]{2,1,0:T(2,128)(2,1)}), bf16[32,2,2560]{2,1,0:T(2,128)(2,1)S(1)}, u32[]{:S(2)}, u32[]{:S(2)}) async-start(bf16[32,2,2560]{2,1,0:T(2,128)(2,1)} %reshape.458), calls=%async_computation.1 | async-start | bytes 655360 | tf_op jit(solution)/shard_map/while/body/eval_jaxpr/all_to_all | solution.py:103
  470.6 6.4 collective-permute-start
  477.3 21.9 %copy-start = (bf16[1,1,256,2560]{3,2,1,0:T(8,128)(2,1)S(1)}, bf16[1,1,256,2560]{3,2,1,0:T(8,128)(2,1)}, u32[]{:S(2)}) copy-start(bf16[1,1,256,2560]{3,2,1,0:T(8,128)(2,1)} %get-tuple-element.660) | copy-start | bytes 3932164 | tf_op jit(solution)/shard_map/while
  478.2 16.3 %all-to-all-start = ((bf16[32,2,2560]{2,1,0:T(2,128)(2,1)}), bf16[32,2,2560]{2,1,0:T(2,128)(2,1)S(1)}, u32[]{:S(2)}, u32[]{:S(2)}) async-start(bf16[32,2,2560]{2,1,0:T(2,128)(2,1)} %bitcast.270), calls=%async_computation | async-start | bytes 655360 | tf_op jit(solution)/shard_map/while/body/eval_jaxpr/all_to_all | solution.py:82
  503.4 15.1 %all-to-all-start.1 = ((bf16[32,2,2560]{2,1,0:T(2,128)(2,1)}), bf16[32,2,2560]{2,1,0:T(2,128)(2,1)S(1)}, u32[]{:S(2)}, u32[]{:S(2)}) async-start(bf16[32,2,2560]{2,1,0:T(2,128)(2,1)} %reshape.458), calls=%async_computation.1 | async-start | bytes 655360 | tf_op jit(solution)/shard_map/while/body/eval_jaxpr/all_to_all | solution.py:103
  521.6 8.1 collective-permute-start
  529.8 22.0 %copy-start.1 = (bf16[1,1,256,2560]{3,2,1,0:T(8,128)(2,1)S(1)}, bf16[1,1,256,2560]{3,2,1,0:T(8,128)(2,1)}, u32[]{:S(2)}) copy-start(bf16[1,1,256,2560]{3,2,1,0:T(8,128)(2,1)} %get-tuple-element.661) | copy-start | bytes 3932164 | tf_op jit(solution)/shard_map/while
  530.0 24.5 %copy-start = (bf16[1,1,256,2560]{3,2,1,0:T(8,128)(2,1)S(1)}, bf16[1,1,256,2560]{3,2,1,0:T(8,128)(2,1)}, u32[]{:S(2)}) copy-start(bf16[1,1,256,2560]{3,2,1,0:T(8,128)(2,1)} %get-tuple-element.660) | copy-start | bytes 3932164 | tf_op jit(solution)/shard_map/while
  530.9 18.9 %all-to-all-start = ((bf16[32,2,2560]{2,1,0:T(2,128)(2,1)}), bf16[32,2,2560]{2,1,0:T(2,128)(2,1)S(1)}, u32[]{:S(2)}, u32[]{:S(2)}) async-start(bf16[32,2,2560]{2,1,0:T(2,128)(2,1)} %bitcast.270), calls=%async_computation | async-start | bytes 655360 | tf_op jit(solution)/shard_map/while/body/eval_jaxpr/all_to_all | solution.py:82
  558.7 15.4 %all-to-all-start.1 = ((bf16[32,2,2560]{2,1,0:T(2,128)(2,1)}), bf16[32,2,2560]{2,1,0:T(2,128)(2,1)S(1)}, u32[]{:S(2)}, u32[]{:S(2)}) async-start(bf16[32,2,2560]{2,1,0:T(2,128)(2,1)} %reshape.458), calls=%async_computation.1 | async-start | bytes 655360 | tf_op jit(solution)/shard_map/while/body/eval_jaxpr/all_to_all | solution.py:103
  577.3 5.2 collective-permute-start
  582.7 21.1 %copy-start = (bf16[1,1,256,2560]{3,2,1,0:T(8,128)(2,1)S(1)}, bf16[1,1,256,2560]{3,2,1,0:T(8,128)(2,1)}, u32[]{:S(2)}) copy-start(bf16[1,1,256,2560]{3,2,1,0:T(8,128)(2,1)} %get-tuple-element.660) | copy-start | bytes 3932164 | tf_op jit(solution)/shard_map/while
  583.6 15.5 %all-to-all-start = ((bf16[32,2,2560]{2,1,0:T(2,128)(2,1)}), bf16[32,2,2560]{2,1,0:T(2,128)(2,1)S(1)}, u32[]{:S(2)}, u32[]{:S(2)}) async-start(bf16[32,2,2560]{2,1,0:T(2,128)(2,1)} %bitcast.270), calls=%async_computation | async-start | bytes 655360 | tf_op jit(solution)/shard_map/while/body/eval_jaxpr/all_to_all | solution.py:82
  608.1 14.9 %all-to-all-start.1 = ((bf16[32,2,2560]{2,1,0:T(2,128)(2,1)}), bf16[32,2,2560]{2,1,0:T(2,128)(2,1)S(1)}, u32[]{:S(2)}, u32[]{:S(2)}) async-start(bf16[32,2,2560]{2,1,0:T(2,128)(2,1)} %reshape.458), calls=%async_computation.1 | async-start | bytes 655360 | tf_op jit(solution)/shard_map/while/body/eval_jaxpr/all_to_all | solution.py:103
  626.2 5.2 collective-permute-start
  631.6 20.4 %copy-start = (bf16[1,1,256,2560]{3,2,1,0:T(8,128)(2,1)S(1)}, bf16[1,1,256,2560]{3,2,1,0:T(8,128)(2,1)}, u32[]{:S(2)}) copy-start(bf16[1,1,256,2560]{3,2,1,0:T(8,128)(2,1)} %get-tuple-element.660) | copy-start | bytes 3932164 | tf_op jit(solution)/shard_map/while
  632.5 14.8 %all-to-all-start = ((bf16[32,2,2560]{2,1,0:T(2,128)(2,1)}), bf16[32,2,2560]{2,1,0:T(2,128)(2,1)S(1)}, u32[]{:S(2)}, u32[]{:S(2)}) async-start(bf16[32,2,2560]{2,1,0:T(2,128)(2,1)} %bitcast.270), calls=%async_computation | async-start | bytes 655360 | tf_op jit(solution)/shard_map/while/body/eval_jaxpr/all_to_all | solution.py:82
  656.2 14.7 %all-to-all-start.1 = ((bf16[32,2,2560]{2,1,0:T(2,128)(2,1)}), bf16[32,2,2560]{2,1,0:T(2,128)(2,1)S(1)}, u32[]{:S(2)}, u32[]{:S(2)}) async-start(bf16[32,2,2560]{2,1,0:T(2,128)(2,1)} %reshape.458), calls=%async_computation.1 | async-start | bytes 655360 | tf_op jit(solution)/shard_map/while/body/eval_jaxpr/all_to_all | solution.py:103
  674.1 6.0 collective-permute-start
  681.3 14.8 %all-to-all-start = ((bf16[32,2,2560]{2,1,0:T(2,128)(2,1)}), bf16[32,2,2560]{2,1,0:T(2,128)(2,1)S(1)}, u32[]{:S(2)}, u32[]{:S(2)}) async-start(bf16[32,2,2560]{2,1,0:T(2,128)(2,1)} %bitcast.270), calls=%async_computation | async-start | bytes 655360 | tf_op jit(solution)/shard_map/while/body/eval_jaxpr/all_to_all | solution.py:82
  705.0 14.7 %all-to-all-start.1 = ((bf16[32,2,2560]{2,1,0:T(2,128)(2,1)}), bf16[32,2,2560]{2,1,0:T(2,128)(2,1)S(1)}, u32[]{:S(2)}, u32[]{:S(2)}) async-start(bf16[32,2,2560]{2,1,0:T(2,128)(2,1)} %reshape.458), calls=%async_computation.1 | async-start | bytes 655360 | tf_op jit(solution)/shard_map/while/body/eval_jaxpr/all_to_all | solution.py:103
  722.9 8.3 collective-permute-start
  731.4 20.7 %copy-start = (bf16[1,1,256,2560]{3,2,1,0:T(8,128)(2,1)S(1)}, bf16[1,1,256,2560]{3,2,1,0:T(8,128)(2,1)}, u32[]{:S(2)}) copy-start(bf16[1,1,256,2560]{3,2,1,0:T(8,128)(2,1)} %get-tuple-element.660) | copy-start | bytes 3932164 | tf_op jit(solution)/shard_map/while
  732.3 15.2 %all-to-all-start = ((bf16[32,2,2560]{2,1,0:T(2,128)(2,1)}), bf16[32,2,2560]{2,1,0:T(2,128)(2,1)S(1)}, u32[]{:S(2)}, u32[]{:S(2)}) async-start(bf16[32,2,2560]{2,1,0:T(2,128)(2,1)} %bitcast.270), calls=%async_computation | async-start | bytes 655360 | tf_op jit(solution)/shard_map/while/body/eval_jaxpr/all_to_all | solution.py:82
  756.4 15.1 %all-to-all-start.1 = ((bf16[32,2,2560]{2,1,0:T(2,128)(2,1)}), bf16[32,2,2560]{2,1,0:T(2,128)(2,1)S(1)}, u32[]{:S(2)}, u32[]{:S(2)}) async-start(bf16[32,2,2560]{2,1,0:T(2,128)(2,1)} %reshape.458), calls=%async_computation.1 | async-start | bytes 655360 | tf_op jit(solution)/shard_map/while/body/eval_jaxpr/all_to_all | solution.py:103
  774.6 6.8 collective-permute-start
  781.6 20.8 %copy-start = (bf16[1,1,256,2560]{3,2,1,0:T(8,128)(2,1)S(1)}, bf16[1,1,256,2560]{3,2,1,0:T(8,128)(2,1)}, u32[]{:S(2)}) copy-start(bf16[1,1,256,2560]{3,2,1,0:T(8,128)(2,1)} %get-tuple-element.660) | copy-start | bytes 3932164 | tf_op jit(solution)/shard_map/while
  782.5 15.2 %all-to-all-start = ((bf16[32,2,2560]{2,1,0:T(2,128)(2,1)}), bf16[32,2,2560]{2,1,0:T(2,128)(2,1)S(1)}, u32[]{:S(2)}, u32[]{:S(2)}) async-start(bf16[32,2,2560]{2,1,0:T(2,128)(2,1)} %bitcast.270), calls=%async_computation | async-start | bytes 655360 | tf_op jit(solution)/shard_map/while/body/eval_jaxpr/all_to_all | solution.py:82
  806.6 15.1 %all-to-all-start.1 = ((bf16[32,2,2560]{2,1,0:T(2,128)(2,1)}), bf16[32,2,2560]{2,1,0:T(2,128)(2,1)S(1)}, u32[]{:S(2)}, u32[]{:S(2)}) async-start(bf16[32,2,2560]{2,1,0:T(2,128)(2,1)} %reshape.458), calls=%async_computation.1 | async-start | bytes 655360 | tf_op jit(solution)/shard_map/while/body/eval_jaxpr/all_to_all | solution.py:103
  824.9 5.6 collective-permute-start
  830.7 20.7 %copy-start = (bf16[1,1,256,2560]{3,2,1,0:T(8,128)(2,1)S(1)}, bf16[1,1,256,2560]{3,2,1,0:T(8,128)(2,1)}, u32[]{:S(2)}) copy-start(bf16[1,1,256,2560]{3,2,1,0:T(8,128)(2,1)} %get-tuple-element.660) | copy-start | bytes 3932164 | tf_op jit(solution)/shard_map/while
  831.7 15.2 %all-to-all-start = ((bf16[32,2,2560]{2,1,0:T(2,128)(2,1)}), bf16[32,2,2560]{2,1,0:T(2,128)(2,1)S(1)}, u32[]{:S(2)}, u32[]{:S(2)}) async-start(bf16[32,2,2560]{2,1,0:T(2,128)(2,1)} %bitcast.270), calls=%async_computation | async-start | bytes 655360 | tf_op jit(solution)/shard_map/while/body/eval_jaxpr/all_to_all | solution.py:82
  855.7 16.2 %all-to-all-start.1 = ((bf16[32,2,2560]{2,1,0:T(2,128)(2,1)}), bf16[32,2,2560]{2,1,0:T(2,128)(2,1)S(1)}, u32[]{:S(2)}, u32[]{:S(2)}) async-start(bf16[32,2,2560]{2,1,0:T(2,128)(2,1)} %reshape.458), calls=%async_computation.1 | async-start | bytes 655360 | tf_op jit(solution)/shard_map/while/body/eval_jaxpr/all_to_all | solution.py:103
  875.2 6.6 collective-permute-start
  885.7 91.4 %reduce-scatter.3.cloned.1.call-start = ((), (), s32[]{:S(2)}) async-start(), calls=%async_computation.8 | async-start | bytes 1966080 | tf_op jit(solution)/shard_map/reduce_scatter | solution.py:153
  (52 other events, 643.8 us)
Sparse Core Ops, SparseCore 0:
  50.8 23.6 all-gather.3
  76.6 18.8 all-gather.5
  97.6 18.8 all-gather.7
  885.8 69.8 reduce-scatter.4
  959.0 18.1 reduce-scatter.2
